TPU v7x, 32 devices: a whole 2x2x4 slice. The times are simulated.
32 devices in a mesh: row: 4 (over y, core), col: 8 (over z, x).
Axes of the slice: x: 2, y: 2, z: 4, core: 2. Of those that a mesh axis runs over, the one named last changes fastest.
Arguments:
- left_panel: bfloat16 [256, 512, 32], P('col', 'row'), may hold values from -6 to 6
- right_panel: bfloat16 [256, 512, 32], P('row', 'col'), may hold values from -6 to 6
- pair_grad: bfloat16 [512, 512, 128], P('row', 'col'), may hold values from -24 to 24
- out_weight: bfloat16 [1024, 128], replicated, may hold values from -0.1875 to 0.1875
Outputs:
- left_grad: float32 [256, 512, 32], P('col', 'row')
- right_grad: float32 [256, 512, 32], P('row', 'col')
- weight_grad: float32 [1024, 128], replicated
All inputs are finite; a program needn't handle non-finite values.
Results may differ from a plain program's by a relative error of at most 0.0033.
Values may be sent and summed in bfloat16 or wider, within the bound.
No kernel may reach another device: no remote copies, remote signals or barrier semaphores. Data moves between devices by JAX's collectives and lax.ppermute only.
A program may use at most 64 MiB of HBM per device.

v0:
```python
import jax
import jax.numpy as jnp
from jax import lax
from jax.sharding import PartitionSpec as P

N = 512


def per_device(left_panel, right_panel, pair_grad, out_weight):
    whole_left = lax.all_gather(left_panel, "col", axis=0, tiled=True)
    whole_right = lax.all_gather(right_panel, "row", axis=0, tiled=True)
    sequences, rows_here, channels = whole_left.shape
    cols_here = whole_right.shape[1]
    pair_width = pair_grad.shape[2]
    block_rows = 16
    blocks_total = rows_here // block_rows
    right_flat = whole_right.reshape(sequences, cols_here * channels)
    weight_t = out_weight.T

    def advance(carried, block_index):
        right_acc, weight_acc = carried
        first_row = block_index * block_rows
        grad_rows = lax.dynamic_slice_in_dim(pair_grad, first_row, block_rows, 0).reshape(
            block_rows * cols_here, pair_width
        )
        left_rows = lax.dynamic_slice_in_dim(whole_left, first_row, block_rows, 1).reshape(
            sequences, block_rows * channels
        )
        expanded = (
            jnp.dot(grad_rows, weight_t, preferred_element_type=jnp.float32) / sequences
        ).astype(jnp.bfloat16)
        expanded = (
            expanded.reshape(block_rows, cols_here, channels, channels)
            .transpose(0, 2, 1, 3)
            .reshape(block_rows * channels, cols_here * channels)
        )
        left_term = lax.dot_general(
            right_flat, expanded, (((1,), (1,)), ((), ())), preferred_element_type=jnp.float32
        )
        right_acc = right_acc + jnp.dot(left_rows, expanded, preferred_element_type=jnp.float32)
        outer_prod = lax.dot_general(
            left_rows, right_flat, (((0,), (0,)), ((), ())), preferred_element_type=jnp.float32
        )
        outer_prod = (outer_prod / sequences).astype(jnp.bfloat16)
        outer_prod = (
            outer_prod.reshape(block_rows, channels, cols_here, channels)
            .transpose(0, 2, 1, 3)
            .reshape(block_rows * cols_here, channels * channels)
        )
        weight_acc = weight_acc + lax.dot_general(
            outer_prod, grad_rows, (((0,), (0,)), ((), ())), preferred_element_type=jnp.float32
        )
        return ((right_acc, weight_acc), left_term)

    start_state = (
        jnp.zeros((sequences, cols_here * channels), jnp.float32),
        jnp.zeros(out_weight.shape, jnp.float32),
    )
    (right_acc, weight_acc), left_terms = lax.scan(
        advance, start_state, jnp.arange(blocks_total, dtype=jnp.int32)
    )
    left_terms = lax.psum_scatter(left_terms, "col", scatter_dimension=1, tiled=True)
    left_grad = (
        left_terms.reshape(blocks_total, -1, block_rows, channels)
        .transpose(1, 0, 2, 3)
        .reshape(-1, rows_here, channels)
    )
    right_grad = lax.psum_scatter(right_acc, "row", scatter_dimension=0, tiled=True).reshape(
        -1, cols_here, channels
    )
    weight_total = lax.psum(lax.psum(weight_acc, "col"), "row")
    return (left_grad, right_grad, weight_total / N)


def solution(mesh):
    in_specs = (P("col", "row", None), P("row", "col", None), P("row", "col", None), P())
    out_specs = (P("col", "row", None), P("row", "col", None), P())
    return jax.shard_map(
        per_device, mesh=mesh, in_specs=in_specs, out_specs=out_specs, check_vma=False
    )
```

profile of v0, /device:TPU:0, one launch (start us, length us, event | category | flops | bytes accessed | tf_op | source)
XLA Modules:
  0.0 989.1 jit_solution(7688918199630728284)
XLA Ops:
  10.5 24.3 %all-gather.5.cloned.1.call-done = bf16[256,64,32]{1,2,0:T(8,128)(2,1)} async-done(((bf16[64,64,32]{1,2,0:T(8,128)(2,1)}), bf16[256,64,32]{1,2,0:T(8,128)(2,1)}) %all-gather.5.cloned.1.call-update) | async-done | bytes 1048592 | tf_op jit(solution)/shard_map/all_gather | solution.py:11
  34.9 4.1 copy.26
  40.4 45.7 %all-gather.3.cloned.1.call-done = bf16[256,128,32]{1,2,0:T(8,128)(2,1)} async-done(((bf16[32,128,32]{1,2,0:T(8,128)(2,1)}), bf16[256,128,32]{1,2,0:T(8,128)(2,1)}) %all-gather.3.cloned.1.call-update) | async-done | bytes 2097168 | tf_op jit(solution)/shard_map/all_gather | solution.py:10
  86.1 4.9 copy.27
  91.0 656.4 %while.15 = (s32[]{:T(128)}, f32[256,2048]{1,0:T(8,128)}, f32[1024,128]{1,0:T(8,128)}, f32[8,256,512]{2,0,1:T(8,128)}, s32[8]{0:T(128)S(1)}, /*index=5*/bf16[256...) while((s32[]{:T(128)}, f32[256,2048]{1,0:T(8,128)}, ...), condition=%wide.region_1.2_spmd.clone, body=%wide.region_0.1_spmd.clone.sunk | while | flops 2152988672 | bytes 60555524 | solution.py:59
  99.1 4.0 reshape.54
  103.1 8.8 copy.42
  111.8 11.1 %reshape.55 = bf16[512,2048]{1,0:T(8,128)(2,1)S(1)} reshape(bf16[16,32,64,32]{3,2,1,0:T(8,128)(2,1)} %copy.42) | data formatting | bytes 4194304 | tf_op jit(solution)/shard_map/while/body/eval_jaxpr/reshape | solution.py:35
  128.1 10.6 %reshape.56 = bf16[16,32,64,32]{3,2,1,0:T(8,128)(2,1)} reshape(bf16[512,2048]{1,0:T(8,128)(2,1)} %multiply_convert_fusion.5) | data formatting | bytes 4194304 | tf_op jit(solution)/shard_map/while/body/eval_jaxpr/reshape | solution.py:46
  138.6 8.9 copy.43
  147.5 6.5 reshape.57
  160.0 11.5 %dynamic_update_slice.6 = f32[8,256,512]{2,0,1:T(8,128)} dynamic-update-slice(f32[8,256,512]{2,0,1:T(8,128)} %get-tuple-element.198, f32[1,256,512]{2,0,1:T(1,128)S(1)} %copy.44, s32[]{:T(128)} %get-tuple-element.195, s32[]{:T(128)} %constant.6.clone.1..sunk, s32[]{:T(128)} %constant.6.clone.1..sunk) | dynamic-update-slice | bytes 1048580 | tf_op jit(solution)/shard_map/while/body/jit(dynamic_update_index_in_dim)/dynamic_update_slice | solution.py:59
  179.6 4.0 reshape.54
  183.6 8.8 copy.42
  192.4 11.1 %reshape.55 = bf16[512,2048]{1,0:T(8,128)(2,1)S(1)} reshape(bf16[16,32,64,32]{3,2,1,0:T(8,128)(2,1)} %copy.42) | data formatting | bytes 4194304 | tf_op jit(solution)/shard_map/while/body/eval_jaxpr/reshape | solution.py:35
  210.2 10.6 %reshape.56 = bf16[16,32,64,32]{3,2,1,0:T(8,128)(2,1)} reshape(bf16[512,2048]{1,0:T(8,128)(2,1)} %multiply_convert_fusion.5) | data formatting | bytes 4194304 | tf_op jit(solution)/shard_map/while/body/eval_jaxpr/reshape | solution.py:46
  220.8 8.9 copy.43
  229.7 6.5 reshape.57
  242.3 11.5 %dynamic_update_slice.6 = f32[8,256,512]{2,0,1:T(8,128)} dynamic-update-slice(f32[8,256,512]{2,0,1:T(8,128)} %get-tuple-element.198, f32[1,256,512]{2,0,1:T(1,128)S(1)} %copy.44, s32[]{:T(128)} %get-tuple-element.195, s32[]{:T(128)} %constant.6.clone.1..sunk, s32[]{:T(128)} %constant.6.clone.1..sunk) | dynamic-update-slice | bytes 1048580 | tf_op jit(solution)/shard_map/while/body/jit(dynamic_update_index_in_dim)/dynamic_update_slice | solution.py:59
  261.9 4.0 reshape.54
  265.9 8.8 copy.42
  274.6 11.1 %reshape.55 = bf16[512,2048]{1,0:T(8,128)(2,1)S(1)} reshape(bf16[16,32,64,32]{3,2,1,0:T(8,128)(2,1)} %copy.42) | data formatting | bytes 4194304 | tf_op jit(solution)/shard_map/while/body/eval_jaxpr/reshape | solution.py:35
  292.5 10.6 %reshape.56 = bf16[16,32,64,32]{3,2,1,0:T(8,128)(2,1)} reshape(bf16[512,2048]{1,0:T(8,128)(2,1)} %multiply_convert_fusion.5) | data formatting | bytes 4194304 | tf_op jit(solution)/shard_map/while/body/eval_jaxpr/reshape | solution.py:46
  303.1 8.9 copy.43
  312.0 6.5 reshape.57
  324.6 11.5 %dynamic_update_slice.6 = f32[8,256,512]{2,0,1:T(8,128)} dynamic-update-slice(f32[8,256,512]{2,0,1:T(8,128)} %get-tuple-element.198, f32[1,256,512]{2,0,1:T(1,128)S(1)} %copy.44, s32[]{:T(128)} %get-tuple-element.195, s32[]{:T(128)} %constant.6.clone.1..sunk, s32[]{:T(128)} %constant.6.clone.1..sunk) | dynamic-update-slice | bytes 1048580 | tf_op jit(solution)/shard_map/while/body/jit(dynamic_update_index_in_dim)/dynamic_update_slice | solution.py:59
  344.1 4.0 reshape.54
  348.1 8.8 copy.42
  356.9 11.1 %reshape.55 = bf16[512,2048]{1,0:T(8,128)(2,1)S(1)} reshape(bf16[16,32,64,32]{3,2,1,0:T(8,128)(2,1)} %copy.42) | data formatting | bytes 4194304 | tf_op jit(solution)/shard_map/while/body/eval_jaxpr/reshape | solution.py:35
  374.8 10.6 %reshape.56 = bf16[16,32,64,32]{3,2,1,0:T(8,128)(2,1)} reshape(bf16[512,2048]{1,0:T(8,128)(2,1)} %multiply_convert_fusion.5) | data formatting | bytes 4194304 | tf_op jit(solution)/shard_map/while/body/eval_jaxpr/reshape | solution.py:46
  385.3 8.9 copy.43
  394.2 6.5 reshape.57
  406.8 11.5 %dynamic_update_slice.6 = f32[8,256,512]{2,0,1:T(8,128)} dynamic-update-slice(f32[8,256,512]{2,0,1:T(8,128)} %get-tuple-element.198, f32[1,256,512]{2,0,1:T(1,128)S(1)} %copy.44, s32[]{:T(128)} %get-tuple-element.195, s32[]{:T(128)} %constant.6.clone.1..sunk, s32[]{:T(128)} %constant.6.clone.1..sunk) | dynamic-update-slice | bytes 1048580 | tf_op jit(solution)/shard_map/while/body/jit(dynamic_update_index_in_dim)/dynamic_update_slice | solution.py:59
  426.4 4.0 reshape.54
  430.4 8.8 copy.42
  439.2 11.1 %reshape.55 = bf16[512,2048]{1,0:T(8,128)(2,1)S(1)} reshape(bf16[16,32,64,32]{3,2,1,0:T(8,128)(2,1)} %copy.42) | data formatting | bytes 4194304 | tf_op jit(solution)/shard_map/while/body/eval_jaxpr/reshape | solution.py:35
  457.0 10.6 %reshape.56 = bf16[16,32,64,32]{3,2,1,0:T(8,128)(2,1)} reshape(bf16[512,2048]{1,0:T(8,128)(2,1)} %multiply_convert_fusion.5) | data formatting | bytes 4194304 | tf_op jit(solution)/shard_map/while/body/eval_jaxpr/reshape | solution.py:46
  467.6 8.9 copy.43
  476.5 6.5 reshape.57
  489.1 11.5 %dynamic_update_slice.6 = f32[8,256,512]{2,0,1:T(8,128)} dynamic-update-slice(f32[8,256,512]{2,0,1:T(8,128)} %get-tuple-element.198, f32[1,256,512]{2,0,1:T(1,128)S(1)} %copy.44, s32[]{:T(128)} %get-tuple-element.195, s32[]{:T(128)} %constant.6.clone.1..sunk, s32[]{:T(128)} %constant.6.clone.1..sunk) | dynamic-update-slice | bytes 1048580 | tf_op jit(solution)/shard_map/while/body/jit(dynamic_update_index_in_dim)/dynamic_update_slice | solution.py:59
  508.7 4.0 reshape.54
  512.7 8.8 copy.42
  521.4 11.1 %reshape.55 = bf16[512,2048]{1,0:T(8,128)(2,1)S(1)} reshape(bf16[16,32,64,32]{3,2,1,0:T(8,128)(2,1)} %copy.42) | data formatting | bytes 4194304 | tf_op jit(solution)/shard_map/while/body/eval_jaxpr/reshape | solution.py:35
  539.3 10.6 %reshape.56 = bf16[16,32,64,32]{3,2,1,0:T(8,128)(2,1)} reshape(bf16[512,2048]{1,0:T(8,128)(2,1)} %multiply_convert_fusion.5) | data formatting | bytes 4194304 | tf_op jit(solution)/shard_map/while/body/eval_jaxpr/reshape | solution.py:46
  549.9 8.9 copy.43
  558.8 6.5 reshape.57
  571.4 11.5 %dynamic_update_slice.6 = f32[8,256,512]{2,0,1:T(8,128)} dynamic-update-slice(f32[8,256,512]{2,0,1:T(8,128)} %get-tuple-element.198, f32[1,256,512]{2,0,1:T(1,128)S(1)} %copy.44, s32[]{:T(128)} %get-tuple-element.195, s32[]{:T(128)} %constant.6.clone.1..sunk, s32[]{:T(128)} %constant.6.clone.1..sunk) | dynamic-update-slice | bytes 1048580 | tf_op jit(solution)/shard_map/while/body/jit(dynamic_update_index_in_dim)/dynamic_update_slice | solution.py:59
  590.9 4.0 reshape.54
  594.9 8.8 copy.42
  603.7 11.1 %reshape.55 = bf16[512,2048]{1,0:T(8,128)(2,1)S(1)} reshape(bf16[16,32,64,32]{3,2,1,0:T(8,128)(2,1)} %copy.42) | data formatting | bytes 4194304 | tf_op jit(solution)/shard_map/while/body/eval_jaxpr/reshape | solution.py:35
  621.6 10.6 %reshape.56 = bf16[16,32,64,32]{3,2,1,0:T(8,128)(2,1)} reshape(bf16[512,2048]{1,0:T(8,128)(2,1)} %multiply_convert_fusion.5) | data formatting | bytes 4194304 | tf_op jit(solution)/shard_map/while/body/eval_jaxpr/reshape | solution.py:46
  632.1 8.9 copy.43
  641.0 6.5 reshape.57
  653.6 11.5 %dynamic_update_slice.6 = f32[8,256,512]{2,0,1:T(8,128)} dynamic-update-slice(f32[8,256,512]{2,0,1:T(8,128)} %get-tuple-element.198, f32[1,256,512]{2,0,1:T(1,128)S(1)} %copy.44, s32[]{:T(128)} %get-tuple-element.195, s32[]{:T(128)} %constant.6.clone.1..sunk, s32[]{:T(128)} %constant.6.clone.1..sunk) | dynamic-update-slice | bytes 1048580 | tf_op jit(solution)/shard_map/while/body/jit(dynamic_update_index_in_dim)/dynamic_update_slice | solution.py:59
  677.2 8.8 copy.42
  686.0 11.1 %reshape.55 = bf16[512,2048]{1,0:T(8,128)(2,1)S(1)} reshape(bf16[16,32,64,32]{3,2,1,0:T(8,128)(2,1)} %copy.42) | data formatting | bytes 4194304 | tf_op jit(solution)/shard_map/while/body/eval_jaxpr/reshape | solution.py:35
  703.8 10.6 %reshape.56 = bf16[16,32,64,32]{3,2,1,0:T(8,128)(2,1)} reshape(bf16[512,2048]{1,0:T(8,128)(2,1)} %multiply_convert_fusion.5) | data formatting | bytes 4194304 | tf_op jit(solution)/shard_map/while/body/eval_jaxpr/reshape | solution.py:46
  714.4 8.9 copy.43
  723.3 6.5 reshape.57
  735.9 11.5 %dynamic_update_slice.6 = f32[8,256,512]{2,0,1:T(8,128)} dynamic-update-slice(f32[8,256,512]{2,0,1:T(8,128)} %get-tuple-element.198, f32[1,256,512]{2,0,1:T(1,128)S(1)} %copy.44, s32[]{:T(128)} %get-tuple-element.195, s32[]{:T(128)} %constant.6.clone.1..sunk, s32[]{:T(128)} %constant.6.clone.1..sunk) | dynamic-update-slice | bytes 1048580 | tf_op jit(solution)/shard_map/while/body/jit(dynamic_update_index_in_dim)/dynamic_update_slice | solution.py:59
  747.5 71.5 %all-reduce.3.cloned.1.call-done = f32[1024,128]{1,0:T(8,128)} async-done(((f32[1024,128]{1,0:T(8,128)}), f32[1024,128]{1,0:T(8,128)}) %all-reduce.3.cloned.1.call-update) | async-done | bytes 524304 | tf_op jit(solution)/shard_map/psum | solution.py:71
  820.1 33.6 %all-reduce.5.cloned.1.call-done = f32[1024,128]{1,0:T(8,128)} async-done(((f32[1024,128]{1,0:T(8,128)}), f32[1024,128]{1,0:T(8,128)}) %all-reduce.5.cloned.1.call-update) | async-done | bytes 524304 | tf_op jit(solution)/shard_map/psum | solution.py:71
  855.6 31.8 %reduce-scatter.7.cloned.1.call-done = f32[64,2048]{1,0:T(8,128)} async-done(((f32[256,2048]{1,0:T(8,128)}), f32[64,2048]{1,0:T(8,128)}) %reduce-scatter.7.cloned.1.call-update) | async-done | bytes 524304
  890.8 88.5 %reduce-scatter.5.cloned.1.call-done = f32[8,32,512]{2,0,1:T(8,128)} async-done(((f32[8,256,512]{2,0,1:T(8,128)}), f32[8,32,512]{2,0,1:T(8,128)}) %reduce-scatter.5.cloned.1.call-update) | async-done | bytes 524304 | tf_op jit(solution)/shard_map/reduce_scatter | solution.py:62
  (136 shorter events, 178.3 us)
Async XLA Ops:
  7.2 27.7 %all-gather.5.cloned.1.call-start = ((), (), s32[]{:S(2)}) async-start(), calls=%async_computation.3 | async-start | bytes 2621440 | tf_op jit(solution)/shard_map/all_gather | solution.py:11
  7.9 78.2 %all-gather.3.cloned.1.call-start = ((), (), s32[]{:S(2)}) async-start(), calls=%async_computation.2 | async-start | bytes 2359296 | tf_op jit(solution)/shard_map/all_gather | solution.py:10
  8.6 810.3 %all-reduce.3.cloned.1.call-start = ((), (), s32[]{:S(2)}) async-start(), calls=%async_computation.5 | async-start | bytes 1048576 | tf_op jit(solution)/shard_map/psum | solution.py:71
  123.9 2.1 copy-start
  154.0 3.2 copy-start.1
  204.5 3.7 copy-start
  236.2 3.3 copy-start.1
  286.7 3.7 copy-start
  318.5 3.3 copy-start.1
  369.0 3.7 copy-start
  400.7 3.3 copy-start.1
  451.2 3.7 copy-start
  483.0 3.3 copy-start.1
  533.5 3.7 copy-start
  565.3 3.3 copy-start.1
  615.8 3.7 copy-start
  647.5 3.3 copy-start.1
  698.0 3.7 copy-start
  729.8 3.3 copy-start.1
  747.4 106.3 %all-reduce.5.cloned.1.call-start = ((), (), s32[]{:S(2)}) async-start(), calls=%async_computation.6 | async-start | bytes 1048576 | tf_op jit(solution)/shard_map/psum | solution.py:71
  819.0 68.5 %reduce-scatter.7.cloned.1.call-start = ((), (), s32[]{:S(2)}) async-start(), calls=%async_computation.7 | async-start | bytes 2621440
  819.5 159.7 %reduce-scatter.5.cloned.1.call-start = ((), (), s32[]{:S(2)}) async-start(), calls=%async_computation.4 | async-start | bytes 4718592 | tf_op jit(solution)/shard_map/reduce_scatter | solution.py:62
Sparse Core Ops, SparseCore 0:
  9.5 25.2 all-gather.4
  37.0 49.0 all-gather.2
  747.5 71.3 all-reduce.2
  821.1 32.5 all-reduce.4
  856.1 31.2 reduce-scatter.6
  890.9 88.2 reduce-scatter.4
where the time goes:
time: 1000 us; the launch traced here: 989 us
  local copies, waits for them, and re-layouts  563 us (56%)
  waiting for transfers between devices  298 us (30%)
  matrix products  107 us (11%)
  between operations  14.2 us (1%)
    psum x2, waiting for transfers between devices, per_device(): weight_total = lax.psum(lax.psum(weight_acc, 'col'), 'row')  105 us
    dynamic_update_slice x16, local copies, waits for them, and re-layouts, per_device(): lax.scan(advance, start_state, jnp.arange(blocks_total, dtype=jnp.int32))  102 us
    reshape x8, local copies, waits for them, and re-layouts, advance(): expanded = expanded.reshape(block_rows, cols_here, channels, channels).tr...  88.8 us
    reduce_scatter x1, waiting for transfers between devices, per_device(): lax.psum_scatter(left_terms, 'col', scatter_dimension=1, tiled=True)  88.5 us
    reshape x8, local copies, waits for them, and re-layouts, advance(): outer_prod.reshape(block_rows, channels, cols_here, channels)  84.5 us
    transpose x8, local copies, waits for them, and re-layouts, advance(): outer_prod = outer_prod.reshape(block_rows, channels, cols_here, channels...  71.3 us
    transpose x8, local copies, waits for them, and re-layouts, advance(): expanded = expanded.reshape(block_rows, cols_here, channels, channels).tr...  70 us
    reshape x8, local copies, waits for them, and re-layouts, advance(): outer_prod = outer_prod.reshape(block_rows, channels, cols_here, channels...  51.9 us
  transfers between devices with their start and end apart: 6, of which 6 were waited for; matrix products, arithmetic and copies ran while one was open for 1% of the time, Pallas kernels for 0%

commit v1 on v0

--- a/solution.py
+++ b/solution.py
@@ -1,17 +1,201 @@
+import functools
+
 import jax
 import jax.numpy as jnp
 from jax import lax
+from jax.experimental import pallas as pl
+from jax.experimental.pallas import tpu as pltpu
 from jax.sharding import PartitionSpec as P
 
-N = 512
-
-
-def per_device(left_panel, right_panel, pair_grad, out_weight):
+LANES = 128
+BLOCK = 16
+BF16 = jnp.bfloat16
+F32 = jnp.float32
+
+
+def cost(flops, moved):
+    return pl.CostEstimate(flops=flops, bytes_accessed=moved, transcendentals=0)
+
+
+def params(mib):
+    return pltpu.CompilerParams(vmem_limit_bytes=mib << 20)
+
+
+def expand_kernel(channels, grad_ref, weight_ref, expanded_ref, turned_ref, wide):
+    rows, block, pair_width = grad_ref.shape
+    wide[...] = grad_ref[...].astype(F32).reshape(rows * block, pair_width)
+
+    def pair_of_columns(step, carry):
+        first = step * 2
+        for half in range(2):
+            turned_ref[first + half] = wide[pl.ds(first + half, rows, stride=block), :].astype(BF16)
+        both = turned_ref[pl.ds(first, 2)].reshape(2 * rows, pair_width)
+        product = lax.dot_general(
+            weight_ref[...], both, (((1,), (1,)), ((), ())), preferred_element_type=F32
+        ).astype(BF16)
+        for half in range(2):
+            for c1 in range(channels):
+                expanded_ref[
+                    pl.ds(pl.multiple_of((first + half) * channels, channels), channels), pl.ds(c1 * rows, rows)
+                ] = product[c1 * channels : (c1 + 1) * channels, half * rows : (half + 1) * rows]
+        return carry
+
+    lax.fori_loop(0, block // 2, pair_of_columns, 0)
+
+
+def expand(pair_grad, out_weight, channels):
+    rows, cols, pair_width = pair_grad.shape
+    width = channels * rows
+    return pl.pallas_call(
+        functools.partial(expand_kernel, channels),
+        grid=(cols // BLOCK,),
+        in_specs=[
+            pl.BlockSpec((rows, BLOCK, pair_width), lambda b: (0, b, 0)),
+            pl.BlockSpec(out_weight.shape, lambda b: (0, 0)),
+        ],
+        out_specs=[
+            pl.BlockSpec((BLOCK * channels, width), lambda b: (b, 0)),
+            pl.BlockSpec((BLOCK, rows, pair_width), lambda b: (b, 0, 0)),
+        ],
+        out_shape=[
+            jax.ShapeDtypeStruct((cols * channels, width), BF16),
+            jax.ShapeDtypeStruct((cols, rows, pair_width), BF16),
+        ],
+        scratch_shapes=[pltpu.VMEM((rows * BLOCK, pair_width), F32)],
+        compiler_params=params(32),
+        cost_estimate=cost(2 * rows * cols * channels * channels * pair_width, 2 * cols * channels * width),
+        name="expand",
+    )(pair_grad, out_weight)
+
+
+def left_kernel(right_ref, expanded_ref, out_ref):
+    out_ref[...] = jnp.dot(right_ref[...], expanded_ref[...], preferred_element_type=F32).astype(out_ref.dtype)
+
+
+def left_product(right_flat, expanded, dtype):
+    sequences, depth = right_flat.shape
+    width = expanded.shape[1]
+    tile = 512
+    return pl.pallas_call(
+        left_kernel,
+        grid=(width // tile,),
+        in_specs=[
+            pl.BlockSpec((sequences, depth), lambda n: (0, 0)),
+            pl.BlockSpec((depth, tile), lambda n: (0, n)),
+        ],
+        out_specs=pl.BlockSpec((sequences, tile), lambda n: (0, n)),
+        out_shape=jax.ShapeDtypeStruct((sequences, width), dtype),
+        compiler_params=params(24),
+        cost_estimate=cost(2 * sequences * depth * width, 2 * depth * width),
+        name="left",
+    )(right_flat, expanded)
+
+
+def right_kernel(left_ref, expanded_ref, out_ref):
+    out_ref[...] = lax.dot_general(
+        left_ref[...], expanded_ref[...], (((1,), (1,)), ((), ())), preferred_element_type=F32
+    ).astype(out_ref.dtype)
+
+
+def right_product(left_flat, expanded, dtype):
+    sequences, width = left_flat.shape
+    depth = expanded.shape[0]
+    tile = 256
+    return pl.pallas_call(
+        right_kernel,
+        grid=(depth // tile,),
+        in_specs=[
+            pl.BlockSpec((sequences, width), lambda n: (0, 0)),
+            pl.BlockSpec((tile, width), lambda n: (n, 0)),
+        ],
+        out_specs=pl.BlockSpec((sequences, tile), lambda n: (0, n)),
+        out_shape=jax.ShapeDtypeStruct((sequences, depth), dtype),
+        compiler_params=params(24),
+        cost_estimate=cost(2 * sequences * depth * width, 2 * depth * width),
+        name="right",
+    )(left_flat, expanded)
+
+
+def weight_kernel(channels, left_ref, right_ref, turned_ref, out_ref, outer, right_t):
+    block, rows, pair_width = turned_ref.shape
+    right_t[...] = right_ref[...].T
+
+    for c1 in range(0, channels, 2):
+        product = jnp.dot(
+            right_t[...], left_ref[:, pl.ds(c1 * rows, 2 * rows)], preferred_element_type=F32
+        ).astype(BF16)
+        for half in range(2):
+            for j in range(block):
+                outer[pl.ds((c1 + half) * channels, channels), pl.ds(j * rows, rows)] = product[
+                    j * channels : (j + 1) * channels, half * rows : (half + 1) * rows
+                ]
+    total = jnp.dot(
+        outer[...], turned_ref[...].reshape(block * rows, pair_width), preferred_element_type=F32
+    )
+
+    @pl.when(pl.program_id(0) == 0)
+    def _():
+        out_ref[...] = total
+
+    @pl.when(pl.program_id(0) != 0)
+    def _():
+        out_ref[...] += total
+
+
+def weight_product(left_flat, right_flat, turned, channels):
+    cols, rows, pair_width = turned.shape
+    sequences, width = left_flat.shape
+    return pl.pallas_call(
+        functools.partial(weight_kernel, channels),
+        grid=(cols // BLOCK,),
+        in_specs=[
+            pl.BlockSpec((sequences, width), lambda b: (0, 0)),
+            pl.BlockSpec((sequences, BLOCK * channels), lambda b: (0, b)),
+            pl.BlockSpec((BLOCK, rows, pair_width), lambda b: (b, 0, 0)),
+        ],
+        out_specs=pl.BlockSpec((channels * channels, pair_width), lambda b: (0, 0)),
+        out_shape=jax.ShapeDtypeStruct((channels * channels, pair_width), F32),
+        scratch_shapes=[
+            pltpu.VMEM((channels * channels, BLOCK * rows), BF16),
+            pltpu.VMEM((BLOCK * channels, sequences), BF16),
+        ],
+        compiler_params=params(24),
+        cost_estimate=cost(4 * sequences * cols * channels * width, 2 * sequences * width),
+        name="weight",
+    )(left_flat, right_flat, turned)
+
+
+def by_tiles(left_panel, right_panel, pair_grad, out_weight):
+    left_here, rows, channels = left_panel.shape
+    right_here, cols, _ = right_panel.shape
+    left_flat = left_panel.transpose(0, 2, 1).reshape(left_here, channels * rows)
+    right_flat = right_panel.reshape(right_here, cols * channels)
+    left_flat = lax.all_gather(left_flat, "col", axis=0, tiled=True)
+    right_flat = lax.all_gather(right_flat, "row", axis=0, tiled=True)
+    sequences = left_flat.shape[0]
+
+    expanded, turned = expand(pair_grad, out_weight, channels)
+    left_terms = left_product(right_flat, expanded, F32)
+    weight_terms = weight_product(left_flat, right_flat, turned, channels)
+    right_terms = right_product(left_flat, expanded, F32)
+
+    scale = 1.0 / sequences
+    left_grad = lax.psum_scatter(left_terms, "col", scatter_dimension=0, tiled=True) * scale
+    left_grad = left_grad.reshape(left_here, channels, rows).transpose(0, 2, 1)
+    right_grad = lax.psum_scatter(right_terms, "row", scatter_dimension=0, tiled=True) * scale
+    right_grad = right_grad.reshape(right_here, cols, channels)
+    residues = rows * lax.axis_size("row")
+    weight_grad = lax.psum(weight_terms, ("row", "col")) * (scale / residues)
+    return left_grad, right_grad, weight_grad
+
+
+def by_blocks(left_panel, right_panel, pair_grad, out_weight):
     whole_left = lax.all_gather(left_panel, "col", axis=0, tiled=True)
     whole_right = lax.all_gather(right_panel, "row", axis=0, tiled=True)
     sequences, rows_here, channels = whole_left.shape
     cols_here = whole_right.shape[1]
     pair_width = pair_grad.shape[2]
+    residues = rows_here * lax.axis_size("row")
     block_rows = 16
     blocks_total = rows_here // block_rows
     right_flat = whole_right.reshape(sequences, cols_here * channels)
@@ -69,7 +253,14 @@
         -1, cols_here, channels
     )
     weight_total = lax.psum(lax.psum(weight_acc, "col"), "row")
-    return (left_grad, right_grad, weight_total / N)
+    return (left_grad, right_grad, weight_total / residues)
+
+
+def per_device(left_panel, right_panel, pair_grad, out_weight):
+    rows, cols = pair_grad.shape[:2]
+    fits = rows % LANES == 0 and cols % BLOCK == 0
+    path = by_tiles if fits else by_blocks
+    return path(left_panel, right_panel, pair_grad, out_weight)
 
 
 def solution(mesh):

time: 1000 us -> 359 us (0.36)
  local copies, waits for them, and re-layouts: 563 us -> 33.4 us
  matrix products: 107 us -> 0 us
  Pallas kernels: 0 us -> 37.4 us
  waiting for transfers between devices: 298 us -> 269 us
    reshape x33 -> x1, local copies, waits for them, and re-layouts: 259 us -> 0.9 us  [by_tiles(): right_flat = right_panel.reshape(right_here, cols * channels)]
    transpose x16 -> x0, local copies, waits for them, and re-layouts: 141 us -> none  [the longest x8 71.3 us: advance(): outer_prod = outer_prod.reshape(block_rows, channels, cols_here, channels...]
    dot_general x40 -> x0, matrix products: 107 us -> none  [the longest x8 28.2 us: advance(): jnp.dot(left_rows, expanded, preferred_element_type=jnp.float32)]
    dynamic_update_slice x16 -> x0, local copies, waits for them, and re-layouts: 102 us -> none  [per_device(): lax.scan(advance, start_state, jnp.arange(blocks_total, dtype=jnp.int32))]
    pallas_call x0 -> x4, Pallas kernels: none -> 37.4 us  [the longest x1 12.3 us: expand(): pl.pallas_call(functools.partial(expand_kernel, channels), grid=(cols //...]
    unnamed x7 -> x5, waiting for transfers between devices: 34.3 us -> 0.08 us
    reduce_scatter x1 -> x2, waiting for transfers between devices: 88.5 us -> 119 us  [the longest x1 88.4 us: by_tiles(): lax.psum_scatter(left_terms, 'col', scatter_dimension=0, tiled=True) * scale]
    convert_element_type x8 -> x0, local copies, waits for them, and re-layouts: 22.8 us -> none  [advance(): expanded = (jnp.dot(grad_rows, weight_t, preferred_element_type=jnp.float...]
  transfers between devices with their start and end apart: 6 -> 5, of which waited for: 6 -> 4; matrix products, arithmetic and copies ran while one was open for 1% -> 2% of each run, Pallas kernels for 0% -> 7%
where the time goes in v1:
time: 359 us; the launch traced here: 358 us
  waiting for transfers between devices  269 us (75%)
  Pallas kernels  37.4 us (10%)
  local copies, waits for them, and re-layouts  33.4 us (9%)
  between operations  13.9 us (4%)
  other arithmetic  4.02 us (1%)
    psum x1, waiting for transfers between devices, by_tiles(): weight_grad = lax.psum(weight_terms, ('row', 'col')) * (scale / residues)  98.7 us
    reduce_scatter x1, waiting for transfers between devices, by_tiles(): lax.psum_scatter(left_terms, 'col', scatter_dimension=0, tiled=True) * scale  88.4 us
    all_gather x1, waiting for transfers between devices, by_tiles(): left_flat = lax.all_gather(left_flat, 'col', axis=0, tiled=True)  51.1 us
    unnamed x30, local copies, waits for them, and re-layouts  32.2 us
    reduce_scatter x1, waiting for transfers between devices, by_tiles(): lax.psum_scatter(right_terms, 'row', scatter_dimension=0, tiled=True)  30.7 us
    pallas_call x1, Pallas kernels, expand(): pl.pallas_call(functools.partial(expand_kernel, channels), grid=(cols //...  12.3 us
    pallas_call x1, Pallas kernels, weight_product(): pl.pallas_call(functools.partial(weight_kernel, channels), grid=(cols //...  11.1 us
    pallas_call x1, Pallas kernels, left_product(): pl.pallas_call(left_kernel, grid=(width // tile,), in_specs=[pl.BlockSpec...  7.34 us
  transfers between devices with their start and end apart: 5, of which 4 were waited for; matrix products, arithmetic and copies ran while one was open for 2% of the time, Pallas kernels for 7%

profile of v1, /device:TPU:0, one launch (start us, length us, event | category | flops | bytes accessed | tf_op | source)
XLA Modules:
  0.0 358.1 jit_solution(4476879955938183468)
XLA Ops:
  7.2 0.0 copy-start.12
  7.2 0.0 copy-start.9
  7.2 0.0 copy-start.8
  7.2 0.0 all-gather.3.cloned.1.call-start
  7.2 2.3 copy.9
  9.5 0.9 copy.10
  10.4 0.0 all-gather.3.cloned.1.call-update
  10.5 0.0 all-gather.5.cloned.1.call-start
  10.5 0.0 copy-done.12
  10.5 0.8 copy.16
  11.3 0.0 all-gather.5.cloned.1.call-update
  11.3 0.0 all-reduce.2.cloned.1.call-start
  11.4 0.0 copy-done.9
  11.4 0.0 copy-done.8
  11.4 12.3 %expand.1 = (bf16[2048,4096]{1,0:T(8,128)(2,1)S(1)}, bf16[64,128,128]{2,1,0:T(8,128)(2,1)S(1)}) custom-call(bf16[128,64,128]{2,1,0:T(8,128)(2,1)S(1)} %copy-done.8, bf16[1024,128]{1,0:T(8,128)(2,1)S(1)} %copy-done.9), custom_call_target="tpu_custom_call" | custom-call | flops 2147483648 | bytes 16777216 | tf_op jit(solution)/shard_map/expand/pallas_call | solution.py:49
  23.7 0.0 copy-start
  23.7 5.7 %copy-done = bf16[2048,4096]{1,0:T(8,128)(2,1)} copy-done((bf16[2048,4096]{1,0:T(8,128)(2,1)}, bf16[2048,4096]{1,0:T(8,128)(2,1)S(1)}, u32[]{:S(2)}) %copy-start) | copy-done | bytes 16777240
  29.4 0.0 copy-start.10
  29.4 1.3 copy-done.10
  30.7 0.0 all-gather.3.cloned.1.call-done.right_ref
  30.7 51.1 %all-gather.5.cloned.1.call-done.left_ref = bf16[256,4096]{1,0:T(8,128)(2,1)} async-done(((bf16[32,4096]{1,0:T(8,128)(2,1)}), bf16[256,4096]{1,0:T(8,128)(2,1)}) %all-gather.5.cloned.1.call-update) | async-done | bytes 2097168 | tf_op jit(solution)/shard_map/all_gather | solution.py:173
  81.9 0.0 copy-start.4
  81.9 1.6 copy-done.4
  83.5 0.0 copy-start.6
  83.5 1.2 copy-done.6
  84.7 0.0 copy-start.11
  84.7 1.6 copy-done.11
  86.3 0.0 copy-start.5
  86.3 11.1 %weight.1 = f32[1024,128]{1,0:T(8,128)} custom-call(bf16[256,4096]{1,0:T(8,128)(2,1)S(1)} %copy-done.4, bf16[256,2048]{1,0:T(8,128)(2,1)S(1)} %copy-done.6, bf16[64,128,128]{2,1,0:T(8,128)(2,1)S(1)} %copy-done.11), custom_call_target="tpu_custom_call" | custom-call | flops 8589934592 | bytes 2097152 | tf_op jit(solution)/shard_map/weight/pallas_call | solution.py:148
  97.3 0.0 all-reduce.2.cloned.1.call-update
  97.4 0.0 reduce-scatter.5.cloned.1.call-start
  97.4 0.0 copy-done.5
  97.4 0.0 copy-start.1
  97.4 5.8 %copy-done.1 = bf16[2048,4096]{1,0:T(8,128)(2,1)S(1)} copy-done((bf16[2048,4096]{1,0:T(8,128)(2,1)S(1)}, bf16[2048,4096]{1,0:T(8,128)(2,1)}, u32[]{:S(2)}) %copy-start.1) | copy-done | bytes 16777240
  103.3 6.8 %right.1 = f32[256,2048]{1,0:T(8,128)} custom-call(bf16[256,4096]{1,0:T(8,128)(2,1)S(1)} %copy-done.5, bf16[2048,4096]{1,0:T(8,128)(2,1)S(1)} %copy-done.1), custom_call_target="tpu_custom_call" | custom-call | flops 4294967296 | bytes 16777216 | tf_op jit(solution)/shard_map/right/pallas_call | solution.py:104
  110.1 0.0 copy-start.7
  110.1 0.0 reduce-scatter.5.cloned.1.call-update
  110.1 0.0 reduce-scatter.3.cloned.1.call-start
  110.1 1.2 copy-done.7
  111.3 0.0 copy-start.2
  111.3 5.8 %copy-done.2 = bf16[2048,4096]{1,0:T(8,128)(2,1)S(1)} copy-done((bf16[2048,4096]{1,0:T(8,128)(2,1)S(1)}, bf16[2048,4096]{1,0:T(8,128)(2,1)}, u32[]{:S(2)}) %copy-start.2) | copy-done | bytes 16777240
  117.1 7.3 %left.1 = f32[256,4096]{1,0:T(8,128)S(1)} custom-call(bf16[256,2048]{1,0:T(8,128)(2,1)S(1)} %copy-done.7, bf16[2048,4096]{1,0:T(8,128)(2,1)S(1)} %copy-done.2), custom_call_target="tpu_custom_call" | custom-call | flops 4294967296 | bytes 16777216 | tf_op jit(solution)/shard_map/left/pallas_call | solution.py:79
  124.5 0.0 copy-start.3
  124.5 1.9 copy-done.3
  126.4 0.0 reduce-scatter.3.cloned.1.call-update
  126.4 98.7 %all-reduce.2.cloned.1.call-done = f32[1024,128]{1,0:T(8,128)} async-done(((f32[1024,128]{1,0:T(8,128)}), f32[1024,128]{1,0:T(8,128)}) %all-reduce.2.cloned.1.call-update) | async-done | bytes 524304 | tf_op jit(solution)/shard_map/psum | solution.py:188
  225.2 1.9 broadcast_multiply_fusion
  227.0 30.7 %reduce-scatter.5.cloned.1.call-done = f32[64,2048]{1,0:T(8,128)} async-done(((f32[256,2048]{1,0:T(8,128)}), f32[64,2048]{1,0:T(8,128)}) %reduce-scatter.5.cloned.1.call-update) | async-done | bytes 524304 | tf_op jit(solution)/shard_map/reduce_scatter | solution.py:185
  257.8 1.1 broadcast_multiply_fusion.1
  258.9 0.3 copy.11
  259.2 2.0 copy.12
  261.2 88.4 %reduce-scatter.3.cloned.1.call-done = f32[32,4096]{1,0:T(8,128)} async-done(((f32[256,4096]{1,0:T(8,128)}), f32[32,4096]{1,0:T(8,128)}) %reduce-scatter.3.cloned.1.call-update) | async-done | bytes 524304 | tf_op jit(solution)/shard_map/reduce_scatter | solution.py:183
  349.6 1.1 multiply_bitcast_fusion
  350.6 0.9 copy.13
Async XLA Ops:
  7.2 3.3 copy-start.12
  7.2 4.2 %copy-start.9 = (bf16[1024,128]{1,0:T(8,128)(2,1)S(1)}, bf16[1024,128]{1,0:T(8,128)(2,1)}, u32[]{:S(2)}) copy-start(bf16[1024,128]{1,0:T(8,128)(2,1)} %weight_ref.1) | copy-start | bytes 786436
  7.2 4.2 %copy-start.8 = (bf16[128,64,128]{2,1,0:T(8,128)(2,1)S(1)}, bf16[128,64,128]{2,1,0:T(8,128)(2,1)}, u32[]{:S(2)}) copy-start(bf16[128,64,128]{2,1,0:T(8,128)(2,1)} %grad_ref.1) | copy-start | bytes 6291460
  7.2 23.5 %all-gather.3.cloned.1.call-start = ((), (), s32[]{:S(2)}) async-start(), calls=%async_computation.2 | async-start | bytes 1310720 | tf_op jit(solution)/shard_map/all_gather | solution.py:174
  10.5 71.4 %all-gather.5.cloned.1.call-start = ((), (), s32[]{:S(2)}) async-start(), calls=%async_computation.4 | async-start | bytes 2359296 | tf_op jit(solution)/shard_map/all_gather | solution.py:173
  11.3 213.8 %all-reduce.2.cloned.1.call-start = ((), (), s32[]{:S(2)}) async-start(), calls=%async_computation.6 | async-start | bytes 1048576 | tf_op jit(solution)/shard_map/psum | solution.py:188
  23.7 5.7 %copy-start = (bf16[2048,4096]{1,0:T(8,128)(2,1)}, bf16[2048,4096]{1,0:T(8,128)(2,1)S(1)}, u32[]{:S(2)}) copy-start(bf16[2048,4096]{1,0:T(8,128)(2,1)S(1)} %get-tuple-element.5.expanded_ref) | copy-start | bytes 50331652
  29.4 1.3 copy-start.10
  81.9 1.6 copy-start.4
  83.5 1.2 copy-start.6
  84.7 1.6 copy-start.11
  86.3 11.1 %copy-start.5 = (bf16[256,4096]{1,0:T(8,128)(2,1)S(1)}, bf16[256,4096]{1,0:T(8,128)(2,1)}, u32[]{:S(2)}) copy-start(bf16[256,4096]{1,0:T(8,128)(2,1)} %all-gather.5.cloned.1.call-done.left_ref) | copy-start | bytes 6291460
  97.4 160.4 %reduce-scatter.5.cloned.1.call-start = ((), (), s32[]{:S(2)}) async-start(), calls=%async_computation.5 | async-start | bytes 2621440 | tf_op jit(solution)/shard_map/reduce_scatter | solution.py:185
  97.4 5.9 %copy-start.1 = (bf16[2048,4096]{1,0:T(8,128)(2,1)S(1)}, bf16[2048,4096]{1,0:T(8,128)(2,1)}, u32[]{:S(2)}) copy-start(bf16[2048,4096]{1,0:T(8,128)(2,1)} %copy-done) | copy-start | bytes 50331652
  110.1 1.2 copy-start.7
  110.1 239.5 %reduce-scatter.3.cloned.1.call-start = ((), (), s32[]{:S(2)}) async-start(), calls=%async_computation.3 | async-start | bytes 4718592 | tf_op jit(solution)/shard_map/reduce_scatter | solution.py:183
  111.3 5.8 %copy-start.2 = (bf16[2048,4096]{1,0:T(8,128)(2,1)S(1)}, bf16[2048,4096]{1,0:T(8,128)(2,1)}, u32[]{:S(2)}) copy-start(bf16[2048,4096]{1,0:T(8,128)(2,1)} %copy-done) | copy-start | bytes 50331652
  124.5 1.9 copy-start.3
Sparse Core Ops, SparseCore 0:
  10.6 19.4 all-gather.2
  32.7 49.0 all-gather.4
  97.5 127.6 all-reduce.1
  227.5 30.1 reduce-scatter.4
  261.2 88.2 reduce-scatter.2

commit v2 on v0

--- a/solution.py
+++ b/solution.py
@@ -1,17 +1,314 @@
 import jax
 import jax.numpy as jnp
 from jax import lax
+from jax.experimental import pallas as pl
+from jax.experimental.pallas import tpu as pltpu
+from jax.sharding import Mesh
 from jax.sharding import PartitionSpec as P
 
-N = 512
-
-
-def per_device(left_panel, right_panel, pair_grad, out_weight):
+LANES = 128
+BLOCK = 16
+BF16 = jnp.bfloat16
+F32 = jnp.float32
+
+
+def cost(flops, moved):
+    return pl.CostEstimate(flops=flops, bytes_accessed=moved, transcendentals=0)
+
+
+def params(mib):
+    return pltpu.CompilerParams(vmem_limit_bytes=mib << 20)
+
+
+def toggled(axis, bit):
+    return [(i, i ^ bit) for i in range(lax.axis_size(axis))]
+
+
+def permute(array, axis, bit):
+    return lax.ppermute(array, axis, toggled(axis, bit))
+
+
+def gather(piece, axis):
+    pieces = {0: piece}
+    for bit in range(2, lax.axis_size(axis), 2):
+        pieces[bit] = permute(piece, axis, bit)
+    for bit in range(0, lax.axis_size(axis), 2):
+        pieces[bit + 1] = permute(pieces[bit], axis, 1)
+    return [pieces[bit] for bit in range(lax.axis_size(axis))]
+
+
+def scatter(slots, axis):
+    size = lax.axis_size(axis)
+    sums = {}
+    for bit in range(0, size, 2):
+        near = permute(slots[bit + 1], axis, 1)
+        sums[bit] = slots[bit].astype(F32) + near.astype(F32)
+    total = sums[0]
+    for bit in range(2, size, 2):
+        total = total + permute(sums[bit].astype(BF16), axis, bit).astype(F32)
+    return total
+
+
+def reduce_everywhere(whole, scale):
+    half = whole.shape[0] // 2
+    mine = lax.axis_index("core")
+    kept = lax.dynamic_slice_in_dim(whole, mine * half, half, 0)
+    sent = lax.dynamic_slice_in_dim(whole, (1 - mine) * half, half, 0)
+    kept = kept + permute(sent, "core", 1)
+    chips = ("far", "col")
+    count = lax.axis_size("far") * lax.axis_size("col")
+    parts = lax.all_to_all(kept.reshape(count, half // count, -1), chips, 0, 0, tiled=True)
+    part = jnp.sum(parts, axis=0) * scale
+    parts = lax.all_to_all(jnp.broadcast_to(part, (count, *part.shape)), chips, 0, 0, tiled=True)
+    kept = parts.reshape(half, -1)
+    other = permute(kept, "core", 1)
+    return jnp.where(mine == 0, jnp.concatenate([kept, other]), jnp.concatenate([other, kept]))
+
+
+def expand(pair_grad, out_weight, channels, blocks, earlier=()):
+    rows, cols, pair_width = pair_grad.shape
+    width = channels * rows
+    first, count = blocks
+    chunk = 8 * channels
+
+    def kernel(*refs):
+        grad_ref, weight_ref, *_, expanded_ref, turned_ref, wide = refs
+        wide[...] = grad_ref[...].astype(F32).reshape(rows * BLOCK, pair_width)
+
+        def pair_of_columns(step, carry):
+            column = step * 2
+            for half in range(2):
+                turned_ref[column + half] = wide[pl.ds(column + half, rows, stride=BLOCK), :].astype(BF16)
+            both = turned_ref[pl.ds(column, 2)].reshape(2 * rows, pair_width)
+            for start in range(0, channels * channels, chunk):
+                product = lax.dot_general(
+                    weight_ref[start : start + chunk, :], both, (((1,), (1,)), ((), ())), preferred_element_type=F32
+                ).astype(BF16)
+                for half in range(2):
+                    row = pl.multiple_of((column + half) * channels, channels)
+                    for c1 in range(chunk // channels):
+                        expanded_ref[pl.ds(row, channels), pl.ds((start // channels + c1) * rows, rows)] = product[
+                            c1 * channels : (c1 + 1) * channels, half * rows : (half + 1) * rows
+                        ]
+            return carry
+
+        lax.fori_loop(0, BLOCK // 2, pair_of_columns, 0, unroll=2)
+
+    return pl.pallas_call(
+        kernel,
+        grid=(count,),
+        in_specs=[
+            pl.BlockSpec((rows, BLOCK, pair_width), lambda b: (0, first + b, 0)),
+            pl.BlockSpec(out_weight.shape, lambda b: (0, 0)),
+        ]
+        + [pl.BlockSpec(memory_space=pl.ANY)] * len(earlier),
+        out_specs=[
+            pl.BlockSpec((BLOCK * channels, width), lambda b: (first + b, 0)),
+            pl.BlockSpec((BLOCK, rows, pair_width), lambda b: (first + b, 0, 0)),
+        ],
+        out_shape=[
+            pltpu.HBM((cols * channels, width), BF16),
+            pltpu.HBM((cols, rows, pair_width), BF16),
+        ],
+        input_output_aliases={2 + n: n for n in range(len(earlier))},
+        scratch_shapes=[pltpu.VMEM((rows * BLOCK, pair_width), F32)],
+        compiler_params=params(16),
+        cost_estimate=cost(
+            4 * rows * count * BLOCK * channels * channels * pair_width, 2 * count * BLOCK * channels * width
+        ),
+        name="expand",
+    )(pair_grad, out_weight, *earlier)
+
+
+def place(pieces, own, target, slot_rows, slot_own):
+    rows = pieces[0].shape[0]
+    unit = min(rows, slot_rows)
+    for bit, piece in enumerate(pieces):
+        for part in range(0, rows, unit):
+            row = (own ^ bit) * rows + part
+            at = ((row // slot_rows) ^ slot_own) * slot_rows + row % slot_rows
+            target[pl.ds(pl.multiple_of(at, unit), unit), :] = piece[part : part + unit, :]
+
+
+def in_hbm(array):
+    return pltpu.with_memory_space_constraint(array, pltpu.HBM)
+
+
+def whole_spec(array):
+    return pl.BlockSpec(array.shape, lambda n: (0,) * array.ndim, pipeline_mode=pl.Buffered(1))
+
+
+def left_product(own, pieces, expanded, slots):
+    sequences = pieces[0].shape[0] * len(pieces)
+    depth, width = expanded.shape
+    tile = 1024
+
+    def kernel(own_ref, *refs):
+        piece_refs, expanded_ref = refs[: len(pieces)], refs[len(pieces)]
+        outs, panel = refs[len(pieces) + 1 : -1], refs[-1]
+        rows = outs[0].shape[0]
+
+        @pl.when(pl.program_id(0) == 0)
+        def _():
+            place(piece_refs, own_ref[0], panel, rows, own_ref[1])
+
+        product = jnp.dot(panel[...], expanded_ref[...], preferred_element_type=F32)
+        for slot, out in enumerate(outs):
+            out[...] = product[slot * rows : (slot + 1) * rows, :].astype(out.dtype)
+
+    return pl.pallas_call(
+        kernel,
+        grid=(width // tile,),
+        in_specs=[pl.BlockSpec(memory_space=pltpu.SMEM)]
+        + [whole_spec(piece) for piece in pieces]
+        + [pl.BlockSpec((depth, tile), lambda n: (0, n))],
+        out_specs=[pl.BlockSpec((sequences // slots, tile), lambda n: (0, n))] * slots,
+        out_shape=[pltpu.HBM((sequences // slots, width), BF16)] * slots,
+        scratch_shapes=[pltpu.VMEM((sequences, depth), BF16)],
+        compiler_params=params(18),
+        cost_estimate=cost(2 * sequences * depth * width, 2 * depth * width),
+        name="left",
+    )(own, *pieces, in_hbm(expanded))
+
+
+def right_product(own, pieces, expanded, slots, after):
+    sequences = pieces[0].shape[0] * len(pieces)
+    depth, width = expanded.shape
+    tile = 512
+
+    def kernel(own_ref, *refs):
+        piece_refs, expanded_ref = refs[: len(pieces)], refs[len(pieces)]
+        outs, panel = refs[len(pieces) + 2 : -1], refs[-1]
+        rows = outs[0].shape[0]
+
+        @pl.when(pl.program_id(0) == 0)
+        def _():
+            place(piece_refs, own_ref[0], panel, rows, own_ref[1])
+
+        product = lax.dot_general(
+            panel[...], expanded_ref[...], (((1,), (1,)), ((), ())), preferred_element_type=F32
+        )
+        for slot, out in enumerate(outs):
+            out[...] = product[slot * rows : (slot + 1) * rows, :].astype(out.dtype)
+
+    return pl.pallas_call(
+        kernel,
+        grid=(depth // tile,),
+        in_specs=[pl.BlockSpec(memory_space=pltpu.SMEM)]
+        + [whole_spec(piece) for piece in pieces]
+        + [pl.BlockSpec((tile, width), lambda n: (n, 0)), pl.BlockSpec(memory_space=pl.ANY)],
+        out_specs=[pl.BlockSpec((sequences // slots, tile), lambda n: (0, n))] * slots,
+        out_shape=[pltpu.HBM((sequences // slots, depth), BF16)] * slots,
+        scratch_shapes=[pltpu.VMEM((sequences, width), BF16)],
+        compiler_params=params(18),
+        cost_estimate=cost(2 * sequences * depth * width, 2 * depth * width),
+        name="right",
+    )(own, *pieces, in_hbm(expanded), after)
+
+
+def weight_product(own, lefts, rights, turned, channels, after):
+    cols, rows, pair_width = turned.shape
+    width = lefts[0].shape[1]
+    sequences = lefts[0].shape[0] * len(lefts)
+
+    def kernel(own_ref, *refs):
+        left_refs, right_refs = refs[: len(lefts)], refs[len(lefts) : len(lefts) + len(rights)]
+        turned_ref, _, out_ref, left, right, right_t, outer = refs[len(lefts) + len(rights) :]
+        step = pl.program_id(0)
+
+        @pl.when(step == 0)
+        def _():
+            place(left_refs, own_ref[1], left, sequences, 0)
+
+        place(right_refs, own_ref[0], right, sequences, 0)
+        right_t[...] = right[...].T
+        for c1 in range(0, channels, 2):
+            product = jnp.dot(
+                right_t[...], left[:, c1 * rows : (c1 + 2) * rows], preferred_element_type=F32
+            ).astype(BF16)
+            for half in range(2):
+                for j in range(BLOCK):
+                    outer[pl.ds((c1 + half) * channels, channels), pl.ds(j * rows, rows)] = product[
+                        j * channels : (j + 1) * channels, half * rows : (half + 1) * rows
+                    ]
+        total = jnp.dot(
+            outer[...], turned_ref[...].reshape(BLOCK * rows, pair_width), preferred_element_type=F32
+        )
+
+        @pl.when(step == 0)
+        def _():
+            out_ref[...] = total
+
+        @pl.when(step != 0)
+        def _():
+            out_ref[...] += total
+
+    block = BLOCK * channels
+    return pl.pallas_call(
+        kernel,
+        grid=(cols // BLOCK,),
+        in_specs=[pl.BlockSpec(memory_space=pltpu.SMEM)]
+        + [whole_spec(piece) for piece in lefts]
+        + [pl.BlockSpec((piece.shape[0], block), lambda b: (0, b)) for piece in rights]
+        + [pl.BlockSpec((BLOCK, rows, pair_width), lambda b: (b, 0, 0)), pl.BlockSpec(memory_space=pl.ANY)],
+        out_specs=pl.BlockSpec((channels * channels, pair_width), lambda b: (0, 0)),
+        out_shape=jax.ShapeDtypeStruct((channels * channels, pair_width), F32),
+        scratch_shapes=[
+            pltpu.VMEM((sequences, width), BF16),
+            pltpu.VMEM((sequences, block), BF16),
+            pltpu.VMEM((block, sequences), BF16),
+            pltpu.VMEM((channels * channels, BLOCK * rows), BF16),
+        ],
+        compiler_params=params(18),
+        cost_estimate=cost(4 * sequences * cols * channels * width, 2 * sequences * width),
+        name="weight",
+    )(own, *lefts, *rights, turned, after)
+
+
+def by_tiles(left_panel, right_panel, pair_grad, out_weight):
+    return tile_plan(left_panel, right_panel, pair_grad, out_weight)
+
+
+def tile_plan(left_panel, right_panel, pair_grad, out_weight):
+    left_here, rows, channels = left_panel.shape
+    right_here, cols, _ = right_panel.shape
+    split_row = ("far", "core")
+    own = jnp.stack([lax.axis_index(split_row), lax.axis_index("col")]).astype(jnp.int32)
+    left_flat = left_panel.transpose(0, 2, 1).reshape(left_here, channels * rows)
+    right_flat = right_panel.reshape(right_here, cols * channels)
+    lefts = gather(left_flat, "col")
+    rights = gather(right_flat, split_row)
+    sequences = left_here * len(lefts)
+    scale = 1.0 / sequences
+
+    lefts, rights = [in_hbm(piece) for piece in lefts], [in_hbm(piece) for piece in rights]
+    pair_grad, out_weight = in_hbm(pair_grad), in_hbm(out_weight)
+    blocks = cols // BLOCK
+    early = blocks // 2
+    arrays = ()
+    if early:
+        arrays = expand(pair_grad, out_weight, channels, (0, early))
+    expanded, turned = expand(pair_grad, out_weight, channels, (early, blocks - early), arrays)
+    left_slots = left_product(own, rights, expanded, len(lefts))
+    weight_terms = weight_product(own, lefts, rights, turned, channels, left_slots[0])
+    right_slots = right_product(own[::-1], lefts, expanded, len(rights), weight_terms)
+
+    left_grad = scatter(left_slots, "col") * scale
+    left_grad = left_grad.reshape(left_here, channels, rows).transpose(0, 2, 1)
+    right_grad = scatter(right_slots, split_row) * scale
+    right_grad = right_grad.reshape(right_here, cols, channels)
+    residues = rows * lax.axis_size(split_row)
+    weight_grad = reduce_everywhere(weight_terms, scale / residues)
+    return left_grad, right_grad, weight_grad
+
+
+def by_blocks(left_panel, right_panel, pair_grad, out_weight):
     whole_left = lax.all_gather(left_panel, "col", axis=0, tiled=True)
     whole_right = lax.all_gather(right_panel, "row", axis=0, tiled=True)
     sequences, rows_here, channels = whole_left.shape
     cols_here = whole_right.shape[1]
     pair_width = pair_grad.shape[2]
+    residues = rows_here * lax.axis_size("row")
     block_rows = 16
     blocks_total = rows_here // block_rows
     right_flat = whole_right.reshape(sequences, cols_here * channels)
@@ -69,12 +366,29 @@
         -1, cols_here, channels
     )
     weight_total = lax.psum(lax.psum(weight_acc, "col"), "row")
-    return (left_grad, right_grad, weight_total / N)
+    return (left_grad, right_grad, weight_total / residues)
+
+
+def powers_of_two(*sizes):
+    return all(size > 1 and size & (size - 1) == 0 for size in sizes)
 
 
 def solution(mesh):
-    in_specs = (P("col", "row", None), P("row", "col", None), P("row", "col", None), P())
-    out_specs = (P("col", "row", None), P("row", "col", None), P())
-    return jax.shard_map(
-        per_device, mesh=mesh, in_specs=in_specs, out_specs=out_specs, check_vma=False
-    )
+    def run(left_panel, right_panel, pair_grad, out_weight):
+        n_row, n_col = mesh.shape["row"], mesh.shape["col"]
+        rows, cols = pair_grad.shape[0] // n_row, pair_grad.shape[1] // n_col
+        tiles = rows == LANES and cols % BLOCK == 0 and powers_of_two(n_row, n_col)
+        if tiles:
+            devices = mesh.devices.reshape(n_row // 2, 2, n_col)
+            used, row, body = Mesh(devices, ("far", "core", "col")), ("far", "core"), by_tiles
+        else:
+            used, row, body = mesh, "row", by_blocks
+        return jax.shard_map(
+            body,
+            mesh=used,
+            in_specs=(P("col", row, None), P(row, "col", None), P(row, "col", None), P()),
+            out_specs=(P("col", row, None), P(row, "col", None), P()),
+            check_vma=False,
+        )(left_panel, right_panel, pair_grad, out_weight)
+
+    return run

time: 1000 us -> 140 us (0.14)
  local copies, waits for them, and re-layouts: 563 us -> 9.88 us
  waiting for transfers between devices: 298 us -> 35.6 us
  matrix products: 107 us -> 0 us
  Pallas kernels: 0 us -> 48.2 us
  starting transfers between devices: 0.23 us -> 36.3 us
  between operations: 14.2 us -> 0.93 us
    reshape x33 -> x1, local copies, waits for them, and re-layouts: 259 us -> 0.2 us  [tile_plan(): right_flat = right_panel.reshape(right_here, cols * channels)]
    transpose x16 -> x0, local copies, waits for them, and re-layouts: 141 us -> none  [the longest x8 71.3 us: advance(): outer_prod = outer_prod.reshape(block_rows, channels, cols_here, channels...]
    dot_general x40 -> x0, matrix products: 107 us -> none  [the longest x8 28.2 us: advance(): jnp.dot(left_rows, expanded, preferred_element_type=jnp.float32)]
    psum x2 -> x0, waiting for transfers between devices: 105 us -> none  [per_device(): weight_total = lax.psum(lax.psum(weight_acc, 'col'), 'row')]
    dynamic_update_slice x16 -> x0, local copies, waits for them, and re-layouts: 102 us -> none  [per_device(): lax.scan(advance, start_state, jnp.arange(blocks_total, dtype=jnp.int32))]
    reduce_scatter x1 -> x0, waiting for transfers between devices: 88.5 us -> none  [per_device(): lax.psum_scatter(left_terms, 'col', scatter_dimension=1, tiled=True)]
    all_gather x2 -> x0, waiting for transfers between devices: 70.1 us -> none  [the longest x1 45.7 us: per_device(): whole_left = lax.all_gather(left_panel, 'col', axis=0, tiled=True)]
    pallas_call x0 -> x5, Pallas kernels: none -> 48.2 us  [the longest x2 15.7 us: expand(): pl.pallas_call(kernel, grid=(count,), in_specs=[pl.BlockSpec((rows, BLOCK...]
  transfers between devices with their start and end apart: 6 -> 24, of which waited for: 6 -> 7; matrix products, arithmetic and copies ran while one was open for 1% -> 8% of each run, Pallas kernels for 0% -> 26%
where the time goes in v2:
time: 140 us; the launch traced here: 138 us
  Pallas kernels  48.2 us (34%)
  starting transfers between devices  36.3 us (26%)
  waiting for transfers between devices  35.6 us (25%)
  local copies, waits for them, and re-layouts  9.88 us (7%)
  other arithmetic  6.85 us (5%)
    ppermute x22, starting transfers between devices, permute(): return lax.ppermute(array, axis, toggled(axis, bit))  24.4 us
    ppermute x22, waiting for transfers between devices, permute(): return lax.ppermute(array, axis, toggled(axis, bit))  17.9 us
    pallas_call x2, Pallas kernels, expand(): pl.pallas_call(kernel, grid=(count,), in_specs=[pl.BlockSpec((rows, BLOCK...  15.7 us
    all_to_all x1, waiting for transfers between devices, reduce_everywhere(): lax.all_to_all(jnp.broadcast_to(part, (count, *part.shape)), chips, 0, 0,...  12.5 us
    pallas_call x1, Pallas kernels, weight_product(): pl.pallas_call(kernel, grid=(cols // BLOCK,), in_specs=[pl.BlockSpec(memo...  12.4 us
    pallas_call x1, Pallas kernels, right_product(): pl.pallas_call(kernel, grid=(depth // tile,), in_specs=[pl.BlockSpec(memo...  10.1 us
    pallas_call x1, Pallas kernels, left_product(): pl.pallas_call(kernel, grid=(width // tile,), in_specs=[pl.BlockSpec(memo...  10.1 us
    unnamed x46, local copies, waits for them, and re-layouts  8.5 us
  transfers between devices with their start and end apart: 24, of which 7 were waited for; matrix products, arithmetic and copies ran while one was open for 8% of the time, Pallas kernels for 26%

profile of v2, /device:TPU:0, one launch (start us, length us, event | category | flops | bytes accessed | tf_op | source)
XLA Modules:
  0.0 137.8 jit_solution(15425054516119862157)
XLA Ops:
  0.6 2.1 %copy.11 = bf16[64,64,32]{0,2,1:T(8,128)(2,1)S(1)} copy(bf16[64,64,32]{1,2,0:T(8,128)(2,1)} %param.5) | data formatting | bytes 524288 | tf_op args[1]
  2.8 0.2 copy.14.refs_0_.refs_8_
  3.0 0.0 copy-start.3
  3.0 3.1 %collective-permute-start.1 = (bf16[64,2048]{1,0:T(8,128)(2,1)S(1)}, bf16[64,2048]{1,0:T(8,128)(2,1)S(1)}, u32[]{:S(2)}, u32[]{:S(2)}) collective-permute-start(bf16[64,2048]{1,0:T(8,128)(2,1)S(1)} %copy.14.refs_0_.refs_8_), channel_id=1, source_target_pairs={{0,16},{8,24},{16,0},{24,8},{1,17},{9,25},{17,1},{25,9},{2,18},{10... | collective-permute-start | bytes 786440 | tf_op jit(solution)/shard_map/ppermute | solution.py:28
  6.0 1.1 copy.21
  7.1 1.6 %collective-permute-start.11 = (bf16[32,4096]{1,0:T(8,128)(2,1)S(1)}, bf16[32,4096]{1,0:T(8,128)(2,1)S(1)}, u32[]{:S(2)}, u32[]{:S(2)}) collective-permute-start(bf16[32,4096]{1,0:T(8,128)(2,1)S(1)} %bitcast.18), channel_id=1, source_target_pairs={{0,2},{1,3},{2,0},{3,1},{4,6},{5,7},{6,4},{7,5},{8,10},{9,11},{10,... | collective-permute-start | bytes 786440 | tf_op jit(solution)/shard_map/ppermute | solution.py:28
  8.8 2.6 %collective-permute-start.13 = (bf16[32,4096]{1,0:T(8,128)(2,1)S(1)}, bf16[32,4096]{1,0:T(8,128)(2,1)S(1)}, u32[]{:S(2)}, u32[]{:S(2)}) collective-permute-start(bf16[32,4096]{1,0:T(8,128)(2,1)S(1)} %bitcast.19), channel_id=1, source_target_pairs={{0,4},{1,5},{2,6},{3,7},{4,0},{5,1},{6,2},{7,3},{8,12},{9,13},{10,... | collective-permute-start | bytes 786440 | tf_op jit(solution)/shard_map/ppermute | solution.py:28
  11.3 0.2 collective-permute-start.15
  11.6 7.9 %expand.2 = (bf16[2048,4096]{1,0:T(8,128)(2,1)}, bf16[64,128,128]{2,1,0:T(8,128)(2,1)}) custom-call(bf16[128,64,128]{2,1,0:T(8,128)(2,1)} %refs_0_.3, bf16[1024,128]{1,0:T(8,128)(2,1)} %refs_1_.3), custom_call_target="tpu_custom_call" | custom-call | flops 2147483648 | bytes 8388608 | tf_op jit(solution)/shard_map/expand/pallas_call | solution.py:97
  19.5 0.0 collective-permute-done.1.refs_2_.refs_10_
  19.5 0.0 copy-start.8
  19.5 0.1 collective-permute-start.2
  19.6 0.1 pad_add_fusion.own_ref
  19.7 0.1 rev.3.own_ref
  19.8 7.8 %expand.3 = (bf16[2048,4096]{1,0:T(8,128)(2,1)}, bf16[64,128,128]{2,1,0:T(8,128)(2,1)}) custom-call(bf16[128,64,128]{2,1,0:T(8,128)(2,1)} %refs_0_.3, bf16[1024,128]{1,0:T(8,128)(2,1)} %refs_1_.3, bf16[2048,4096]{1,0:T(8,128)(2,1)} %get-tuple-element.19.refs_2_, ...), custom_call_target="tpu_custom_call", output_to_operand_aliasing={{0}: (2, {}), {1}: (3, {})} | custom-call | flops 2147483648 | bytes 8388608 | tf_op jit(solution)/shard_map/expand/pallas_call | solution.py:97
  27.6 0.0 copy-start.9
  27.6 1.6 %collective-permute-start.10 = (bf16[32,4096]{1,0:T(8,128)(2,1)S(1)}, bf16[32,4096]{1,0:T(8,128)(2,1)S(1)}, u32[]{:S(2)}, u32[]{:S(2)}) collective-permute-start(bf16[32,4096]{1,0:T(8,128)(2,1)S(1)} %bitcast.21), channel_id=1, source_target_pairs={{0,1},{1,0},{2,3},{3,2},{4,5},{5,4},{6,7},{7,6},{8,9},{9,8},{10,11... | collective-permute-start | bytes 786440 | tf_op jit(solution)/shard_map/ppermute | solution.py:28
  29.2 0.5 collective-permute-start.12
  29.7 0.4 collective-permute-done.13.refs_4_
  30.1 1.5 %collective-permute-start.14 = (bf16[32,4096]{1,0:T(8,128)(2,1)S(1)}, bf16[32,4096]{1,0:T(8,128)(2,1)S(1)}, u32[]{:S(2)}, u32[]{:S(2)}) collective-permute-start(bf16[32,4096]{1,0:T(8,128)(2,1)S(1)} %collective-permute-done.13.refs_4_), channel_id=1, source_target_pairs={{0,1},{1,0},{2,3},{3,2},{4,5},{5,4},{6,7},{7,6},{8,9},{9,8},{10,11... | collective-permute-start | bytes 786440 | tf_op jit(solution)/shard_map/ppermute | solution.py:28
  31.6 0.0 collective-permute-done.15.refs_6_
  31.6 0.5 collective-permute-start.16
  32.2 0.7 copy-done.10
  32.9 10.1 %left.1 = (bf16[32,4096]{1,0:T(8,128)(2,1)}, bf16[32,4096]{1,0:T(8,128)(2,1)}, bf16[32,4096]{1,0:T(8,128)(2,1)}, bf16[32,4096]{1,0:T(8,128)(2,1)}, bf16[32,4096]...) custom-call(s32[2]{0:T(128)S(1)} %pad_add_fusion.own_ref, ...), custom_call_target="tpu_custom_call" | custom-call | flops 4294967296 | bytes 16777216 | tf_op jit(solution)/shard_map/left/pallas_call | solution.py:159
  43.0 0.0 collective-permute-done.12.refs_3_
  43.0 5.1 %collective-permute-done.14.refs_5_ = bf16[32,4096]{1,0:T(8,128)(2,1)S(1)} collective-permute-done((bf16[32,4096]{1,0:T(8,128)(2,1)S(1)}, bf16[32,4096]{1,0:T(8,128)(2,1)S(1)}, u32[]{:S(2)}, u32[]{:S(2)}) %collective-permute-start.14) | collective-permute-done | bytes 262176 | tf_op jit(solution)/shard_map/ppermute | solution.py:28
  48.1 5.1 %collective-permute-done.16.refs_7_ = bf16[32,4096]{1,0:T(8,128)(2,1)S(1)} collective-permute-done((bf16[32,4096]{1,0:T(8,128)(2,1)S(1)}, bf16[32,4096]{1,0:T(8,128)(2,1)S(1)}, u32[]{:S(2)}, u32[]{:S(2)}) %collective-permute-start.16) | collective-permute-done | bytes 262176 | tf_op jit(solution)/shard_map/ppermute | solution.py:28
  53.2 0.7 copy-done.14
  53.9 0.9 copy-done.1
  54.9 12.4 %weight.1.refs_9_ = f32[1024,128]{1,0:T(8,128)S(1)} custom-call(s32[2]{0:T(128)S(1)} %pad_add_fusion.own_ref, bf16[32,4096]{1,0:T(8,128)(2,1)} %bitcast.22, bf16[32,4096]{1,0:T(8,128)(2,1)} %copy-done.11, bf16[32,4096]{1,0:T(8,128)(2,1)} %copy-done.5, bf16[32,4096]{1,0:T(8,128)(2,1)} %copy-done.12, bf16[32,4096]{1,0:T(8,128)(2,1)} %copy-done.6, ...), custom_call_target="tpu_custom_call" | custom-call | flops 8589934592 | bytes 2097152 | tf_op jit(solution)/shard_map/weight/pallas_call | solution.py:247
  67.3 0.1 collective-permute-start.20
  67.4 10.1 %right.1 = (bf16[64,2048]{1,0:T(8,128)(2,1)}, bf16[64,2048]{1,0:T(8,128)(2,1)}, bf16[64,2048]{1,0:T(8,128)(2,1)}, bf16[64,2048]{1,0:T(8,128)(2,1)}) custom-call(s32[2]{0:T(128)S(1)} %rev.3.own_ref, bf16[32,4096]{1,0:T(8,128)(2,1)} %bitcast.23, bf16[32,4096]{1,0:T(8,128)(2,1)} %copy-done.11, bf16[32,4096]{1,0:T(8,128)(2,1)} %copy-done.5, ...), custom_call_target="tpu_custom_call" | custom-call | flops 4294967296 | bytes 16777216 | tf_op jit(solution)/shard_map/right/pallas_call | solution.py:194
  77.5 0.5 collective-permute-start.18
  78.0 0.1 collective-permute-start.17
  78.1 1.5 %collective-permute-start.4 = (bf16[32,4096]{1,0:T(8,128)(2,1)S(1)}, bf16[32,4096]{1,0:T(8,128)(2,1)S(1)}, u32[]{:S(2)}, u32[]{:S(2)}) collective-permute-start(bf16[32,4096]{1,0:T(8,128)(2,1)S(1)} %copy-done.20), channel_id=1, source_target_pairs={{0,1},{1,0},{2,3},{3,2},{4,5},{5,4},{6,7},{7,6},{8,9},{9,8},{10,11... | collective-permute-start | bytes 786440 | tf_op jit(solution)/shard_map/ppermute | solution.py:28
  79.6 0.5 collective-permute-start.6
  80.1 0.0 collective-permute-done.20
  80.1 1.5 %collective-permute-start.8 = (bf16[32,4096]{1,0:T(8,128)(2,1)}, bf16[32,4096]{1,0:T(8,128)(2,1)S(1)}, u32[]{:S(2)}, u32[]{:S(2)}) collective-permute-start(bf16[32,4096]{1,0:T(8,128)(2,1)} %get-tuple-element.29), channel_id=1, source_target_pairs={{0,1},{1,0},{2,3},{3,2},{4,5},{5,4},{6,7},{7,6},{8,9},{9,8},{10,11... | collective-permute-start | bytes 786440 | tf_op jit(solution)/shard_map/ppermute | solution.py:28
  81.6 0.8 dynamic-slice_add_fusion
  82.3 5.1 %all-to-all-start = ((f32[16,32,128]{2,1,0:T(8,128)}), f32[16,32,128]{2,1,0:T(8,128)S(1)}, u32[]{:S(2)}, u32[]{:S(2)}) async-start(f32[16,32,128]{2,1,0:T(8,128)} %bitcast.6), calls=%async_computation | async-start | bytes 524288 | tf_op jit(solution)/shard_map/all_to_all | solution.py:60
  87.5 0.0 collective-permute-done.18
  87.5 2.0 %collective-permute-start.3 = (bf16[32,4096]{1,0:T(8,128)(2,1)}, bf16[32,4096]{1,0:T(8,128)(2,1)S(1)}, u32[]{:S(2)}, u32[]{:S(2)}) collective-permute-start(bf16[32,4096]{1,0:T(8,128)(2,1)} %get-tuple-element.23), channel_id=1, source_target_pairs={{0,1},{1,0},{2,3},{3,2},{4,5},{5,4},{6,7},{7,6},{8,9},{9,8},{10,11... | collective-permute-start | bytes 786440 | tf_op jit(solution)/shard_map/ppermute | solution.py:28
  89.5 1.1 add_convert_fusion
  90.5 0.0 collective-permute-done.4
  90.5 1.5 %collective-permute-start.19 = (bf16[64,2048]{1,0:T(8,128)(2,1)S(1)}, bf16[64,2048]{1,0:T(8,128)(2,1)}, u32[]{:S(2)}, u32[]{:S(2)}) collective-permute-start(bf16[64,2048]{1,0:T(8,128)(2,1)S(1)} %add_convert_fusion), channel_id=1, source_target_pairs={{0,16},{8,24},{16,0},{24,8},{1,17},{9,25},{17,1},{25,9},{2,18},{10... | collective-permute-start | bytes 786440 | tf_op jit(solution)/shard_map/ppermute | solution.py:28
  92.1 0.1 add_convert_fusion.3
  92.1 2.2 %collective-permute-done.6 = bf16[32,4096]{1,0:T(8,128)(2,1)} collective-permute-done((bf16[32,4096]{1,0:T(8,128)(2,1)S(1)}, bf16[32,4096]{1,0:T(8,128)(2,1)}, u32[]{:S(2)}, u32[]{:S(2)}) %collective-permute-start.6) | collective-permute-done | bytes 262176 | tf_op jit(solution)/shard_map/ppermute | solution.py:28
  94.4 0.7 collective-permute-start.5
  95.1 1.0 add_convert_fusion.2
  96.1 5.2 %all-to-all-done = f32[16,32,128]{2,1,0:T(8,128)S(1)} async-done(((f32[16,32,128]{2,1,0:T(8,128)}), f32[16,32,128]{2,1,0:T(8,128)S(1)}, u32[]{:S(2)}, u32[]{:S(2)}) %all-to-all-start) | async-done | bytes 262176 | tf_op jit(solution)/shard_map/all_to_all | solution.py:60
  101.3 0.7 broadcast_in_dim.3
  102.1 6.8 %all-to-all-start.1 = ((f32[16,32,128]{2,1,0:T(8,128)}), f32[16,32,128]{2,1,0:T(8,128)S(1)}, u32[]{:S(2)}, u32[]{:S(2)}) async-start(f32[16,32,128]{2,1,0:T(8,128)} %broadcast_in_dim.3), calls=%async_computation.1 | async-start | bytes 524288 | tf_op jit(solution)/shard_map/all_to_all | solution.py:62
  108.9 0.0 collective-permute-done.8
  108.9 2.9 %collective-permute-start.7 = (bf16[32,4096]{1,0:T(8,128)(2,1)S(1)}, bf16[32,4096]{1,0:T(8,128)(2,1)}, u32[]{:S(2)}, u32[]{:S(2)}) collective-permute-start(bf16[32,4096]{1,0:T(8,128)(2,1)S(1)} %add_convert_fusion.2), channel_id=1, source_target_pairs={{0,4},{1,5},{2,6},{3,7},{4,0},{5,1},{6,2},{7,3},{8,12},{9,13},{10,... | collective-permute-start | bytes 786440 | tf_op jit(solution)/shard_map/ppermute | solution.py:28
  111.8 0.8 add_convert_fusion.1
  112.5 1.5 %collective-permute-start.9 = (bf16[32,4096]{1,0:T(8,128)(2,1)}, bf16[32,4096]{1,0:T(8,128)(2,1)}, u32[]{:S(2)}, u32[]{:S(2)}) collective-permute-start(bf16[32,4096]{1,0:T(8,128)(2,1)} %add_convert_fusion.1), channel_id=1, source_target_pairs={{0,6},{1,7},{2,4},{3,5},{4,2},{5,3},{6,0},{7,1},{8,14},{9,15},{10,... | collective-permute-start | bytes 786440 | tf_op jit(solution)/shard_map/ppermute | solution.py:28
  114.0 1.1 add_multiply_fusion
  115.1 0.3 copy.16
  115.4 2.0 %copy.17 = f32[64,64,32]{1,2,0:T(8,128)} copy(f32[64,64,32]{0,2,1:T(8,128)S(1)} %bitcast.16) | data formatting | bytes 1048576
  117.4 12.5 %all-to-all-done.1 = f32[16,32,128]{2,1,0:T(8,128)S(1)} async-done(((f32[16,32,128]{2,1,0:T(8,128)}), f32[16,32,128]{2,1,0:T(8,128)S(1)}, u32[]{:S(2)}, u32[]{:S(2)}) %all-to-all-start.1) | async-done | bytes 262176 | tf_op jit(solution)/shard_map/all_to_all | solution.py:62
  130.0 5.0 %collective-permute-done.7 = bf16[32,4096]{1,0:T(8,128)(2,1)} collective-permute-done((bf16[32,4096]{1,0:T(8,128)(2,1)S(1)}, bf16[32,4096]{1,0:T(8,128)(2,1)}, u32[]{:S(2)}, u32[]{:S(2)}) %collective-permute-start.7) | collective-permute-done | bytes 262176 | tf_op jit(solution)/shard_map/ppermute | solution.py:28
  134.9 1.2 multiply_bitcast_fusion
  136.1 0.9 copy.18
  137.0 0.8 maximum_select_fusion
  (51 shorter events, 0.2 us)
Async XLA Ops:
  3.0 16.5 %copy-start.3 = (bf16[64,2048]{1,0:T(8,128)(2,1)}, bf16[64,2048]{1,0:T(8,128)(2,1)S(1)}, u32[]{:S(2)}) copy-start(bf16[64,2048]{1,0:T(8,128)(2,1)S(1)} %copy.14.refs_0_.refs_8_) | copy-start | bytes 786436
  3.0 16.5 %collective-permute-start.1 = (bf16[64,2048]{1,0:T(8,128)(2,1)S(1)}, bf16[64,2048]{1,0:T(8,128)(2,1)S(1)}, u32[]{:S(2)}, u32[]{:S(2)}) collective-permute-start(bf16[64,2048]{1,0:T(8,128)(2,1)S(1)} %copy.14.refs_0_.refs_8_), channel_id=1, source_target_pairs={{0,16},{8,24},{16,0},{24,8},{1,17},{9,25},{17,1},{25,9},{2,18},{10... | collective-permute-start | bytes 786440 | tf_op jit(solution)/shard_map/ppermute | solution.py:28
  6.0 21.5 %collective-permute-start = (bf16[64,2048]{1,0:T(8,128)(2,1)S(1)}, bf16[64,2048]{1,0:T(8,128)(2,1)S(1)}, u32[]{:S(2)}, u32[]{:S(2)}) collective-permute-start(bf16[64,2048]{1,0:T(8,128)(2,1)S(1)} %copy.14.refs_0_.refs_8_), channel_id=1, source_target_pairs={{0,8},{8,0},{16,24},{24,16},{1,9},{9,1},{17,25},{25,17},{2,10},{10... | collective-permute-start | bytes 786440 | tf_op jit(solution)/shard_map/ppermute | solution.py:28
  7.1 20.5 %copy-start.4 = (bf16[4,8,32,128]{3,1,2,0:T(8,128)(2,1)}, bf16[4,8,32,128]{3,1,2,0:T(8,128)(2,1)S(1)}, u32[]{:S(2)}) copy-start(bf16[4,8,32,128]{3,1,2,0:T(8,128)(2,1)S(1)} %copy.21) | copy-start | bytes 786436
  7.1 22.0 %collective-permute-start.11 = (bf16[32,4096]{1,0:T(8,128)(2,1)S(1)}, bf16[32,4096]{1,0:T(8,128)(2,1)S(1)}, u32[]{:S(2)}, u32[]{:S(2)}) collective-permute-start(bf16[32,4096]{1,0:T(8,128)(2,1)S(1)} %bitcast.18), channel_id=1, source_target_pairs={{0,2},{1,3},{2,0},{3,1},{4,6},{5,7},{6,4},{7,5},{8,10},{9,11},{10,... | collective-permute-start | bytes 786440 | tf_op jit(solution)/shard_map/ppermute | solution.py:28
  8.8 21.4 %collective-permute-start.13 = (bf16[32,4096]{1,0:T(8,128)(2,1)S(1)}, bf16[32,4096]{1,0:T(8,128)(2,1)S(1)}, u32[]{:S(2)}, u32[]{:S(2)}) collective-permute-start(bf16[32,4096]{1,0:T(8,128)(2,1)S(1)} %bitcast.19), channel_id=1, source_target_pairs={{0,4},{1,5},{2,6},{3,7},{4,0},{5,1},{6,2},{7,3},{8,12},{9,13},{10,... | collective-permute-start | bytes 786440 | tf_op jit(solution)/shard_map/ppermute | solution.py:28
  11.3 20.3 %collective-permute-start.15 = (bf16[32,4096]{1,0:T(8,128)(2,1)S(1)}, bf16[32,4096]{1,0:T(8,128)(2,1)S(1)}, u32[]{:S(2)}, u32[]{:S(2)}) collective-permute-start(bf16[32,4096]{1,0:T(8,128)(2,1)S(1)} %bitcast.20), channel_id=1, source_target_pairs={{0,6},{1,7},{2,4},{3,5},{4,2},{5,3},{6,0},{7,1},{8,14},{9,15},{10,... | collective-permute-start | bytes 786440 | tf_op jit(solution)/shard_map/ppermute | solution.py:28
  19.5 8.1 %copy-start.8 = (bf16[64,2048]{1,0:T(8,128)(2,1)}, bf16[64,2048]{1,0:T(8,128)(2,1)S(1)}, u32[]{:S(2)}) copy-start(bf16[64,2048]{1,0:T(8,128)(2,1)S(1)} %collective-permute-done.1.refs_2_.refs_10_) | copy-start | bytes 786436
  19.5 12.7 %collective-permute-start.2 = (bf16[64,2048]{1,0:T(8,128)(2,1)S(1)}, bf16[64,2048]{1,0:T(8,128)(2,1)S(1)}, u32[]{:S(2)}, u32[]{:S(2)}) collective-permute-start(bf16[64,2048]{1,0:T(8,128)(2,1)S(1)} %collective-permute-done.1.refs_2_.refs_10_), channel_id=1, source_target_pairs={{0,8},{8,0},{16,24},{24,16},{1,9},{9,1},{17,25},{25,17},{2,10},{10... | collective-permute-start | bytes 786440 | tf_op jit(solution)/shard_map/ppermute | solution.py:28
  27.6 4.6 %copy-start.9 = (bf16[64,2048]{1,0:T(8,128)(2,1)}, bf16[64,2048]{1,0:T(8,128)(2,1)S(1)}, u32[]{:S(2)}) copy-start(bf16[64,2048]{1,0:T(8,128)(2,1)S(1)} %collective-permute-done.refs_1_.refs_9_) | copy-start | bytes 786436
  27.6 15.4 %collective-permute-start.10 = (bf16[32,4096]{1,0:T(8,128)(2,1)S(1)}, bf16[32,4096]{1,0:T(8,128)(2,1)S(1)}, u32[]{:S(2)}, u32[]{:S(2)}) collective-permute-start(bf16[32,4096]{1,0:T(8,128)(2,1)S(1)} %bitcast.21), channel_id=1, source_target_pairs={{0,1},{1,0},{2,3},{3,2},{4,5},{5,4},{6,7},{7,6},{8,9},{9,8},{10,11... | collective-permute-start | bytes 786440 | tf_op jit(solution)/shard_map/ppermute | solution.py:28
  29.2 13.8 %copy-start.5 = (bf16[32,4096]{1,0:T(8,128)(2,1)}, bf16[32,4096]{1,0:T(8,128)(2,1)S(1)}, u32[]{:S(2)}) copy-start(bf16[32,4096]{1,0:T(8,128)(2,1)S(1)} %collective-permute-done.11.refs_2_) | copy-start | bytes 786436
  29.2 13.8 %collective-permute-start.12 = (bf16[32,4096]{1,0:T(8,128)(2,1)S(1)}, bf16[32,4096]{1,0:T(8,128)(2,1)S(1)}, u32[]{:S(2)}, u32[]{:S(2)}) collective-permute-start(bf16[32,4096]{1,0:T(8,128)(2,1)S(1)} %collective-permute-done.11.refs_2_), channel_id=1, source_target_pairs={{0,1},{1,0},{2,3},{3,2},{4,5},{5,4},{6,7},{7,6},{8,9},{9,8},{10,11... | collective-permute-start | bytes 786440 | tf_op jit(solution)/shard_map/ppermute | solution.py:28
  30.1 12.8 %copy-start.6 = (bf16[32,4096]{1,0:T(8,128)(2,1)}, bf16[32,4096]{1,0:T(8,128)(2,1)S(1)}, u32[]{:S(2)}) copy-start(bf16[32,4096]{1,0:T(8,128)(2,1)S(1)} %collective-permute-done.13.refs_4_) | copy-start | bytes 786436
  30.1 18.0 %collective-permute-start.14 = (bf16[32,4096]{1,0:T(8,128)(2,1)S(1)}, bf16[32,4096]{1,0:T(8,128)(2,1)S(1)}, u32[]{:S(2)}, u32[]{:S(2)}) collective-permute-start(bf16[32,4096]{1,0:T(8,128)(2,1)S(1)} %collective-permute-done.13.refs_4_), channel_id=1, source_target_pairs={{0,1},{1,0},{2,3},{3,2},{4,5},{5,4},{6,7},{7,6},{8,9},{9,8},{10,11... | collective-permute-start | bytes 786440 | tf_op jit(solution)/shard_map/ppermute | solution.py:28
  31.6 11.3 %copy-start.7 = (bf16[32,4096]{1,0:T(8,128)(2,1)}, bf16[32,4096]{1,0:T(8,128)(2,1)S(1)}, u32[]{:S(2)}) copy-start(bf16[32,4096]{1,0:T(8,128)(2,1)S(1)} %collective-permute-done.15.refs_6_) | copy-start | bytes 786436
  31.6 21.6 %collective-permute-start.16 = (bf16[32,4096]{1,0:T(8,128)(2,1)S(1)}, bf16[32,4096]{1,0:T(8,128)(2,1)S(1)}, u32[]{:S(2)}, u32[]{:S(2)}) collective-permute-start(bf16[32,4096]{1,0:T(8,128)(2,1)S(1)} %collective-permute-done.15.refs_6_), channel_id=1, source_target_pairs={{0,1},{1,0},{2,3},{3,2},{4,5},{5,4},{6,7},{7,6},{8,9},{9,8},{10,11... | collective-permute-start | bytes 786440 | tf_op jit(solution)/shard_map/ppermute | solution.py:28
  32.2 0.7 copy-start.10
  32.9 21.1 %copy-start = (bf16[64,128,128]{2,1,0:T(8,128)(2,1)S(1)}, bf16[64,128,128]{2,1,0:T(8,128)(2,1)}, u32[]{:S(2)}) copy-start(bf16[64,128,128]{2,1,0:T(8,128)(2,1)} %get-tuple-element.30.refs_12_) | copy-start | bytes 6291460
  43.0 10.2 %copy-start.11 = (bf16[32,4096]{1,0:T(8,128)(2,1)}, bf16[32,4096]{1,0:T(8,128)(2,1)S(1)}, u32[]{:S(2)}) copy-start(bf16[32,4096]{1,0:T(8,128)(2,1)S(1)} %collective-permute-done.10.refs_1_) | copy-start | bytes 786436
  43.0 10.2 %copy-start.12 = (bf16[32,4096]{1,0:T(8,128)(2,1)}, bf16[32,4096]{1,0:T(8,128)(2,1)S(1)}, u32[]{:S(2)}) copy-start(bf16[32,4096]{1,0:T(8,128)(2,1)S(1)} %collective-permute-done.12.refs_3_) | copy-start | bytes 786436
  48.1 5.2 %copy-start.13 = (bf16[32,4096]{1,0:T(8,128)(2,1)}, bf16[32,4096]{1,0:T(8,128)(2,1)S(1)}, u32[]{:S(2)}) copy-start(bf16[32,4096]{1,0:T(8,128)(2,1)S(1)} %collective-permute-done.14.refs_5_) | copy-start | bytes 786436
  53.2 0.7 copy-start.14
  53.9 1.0 copy-start.1
  67.3 10.8 %copy-start.20 = (bf16[32,4096]{1,0:T(8,128)(2,1)S(1)}, bf16[32,4096]{1,0:T(8,128)(2,1)}, u32[]{:S(2)}) copy-start(bf16[32,4096]{1,0:T(8,128)(2,1)} %get-tuple-element.25) | copy-start | bytes 786436
  67.3 12.3 %copy-start.19 = (bf16[32,4096]{1,0:T(8,128)(2,1)S(1)}, bf16[32,4096]{1,0:T(8,128)(2,1)}, u32[]{:S(2)}) copy-start(bf16[32,4096]{1,0:T(8,128)(2,1)} %get-tuple-element.27) | copy-start | bytes 786436
  67.3 12.8 %collective-permute-start.20 = (f32[512,128]{1,0:T(8,128)S(1)}, f32[512,128]{1,0:T(8,128)S(1)}, u32[]{:S(2)}, u32[]{:S(2)}) collective-permute-start(f32[512,128]{1,0:T(8,128)S(1)} %constant_dynamic-slice_fusion), channel_id=1, source_target_pairs={{0,8},{8,0},{1,9},{9,1},{2,10},{10,2},{3,11},{11,3},{4,12},{12,4},... | collective-permute-start | bytes 786440 | tf_op jit(solution)/shard_map/ppermute | solution.py:28
  77.5 14.6 %copy-start.18 = (bf16[32,4096]{1,0:T(8,128)(2,1)S(1)}, bf16[32,4096]{1,0:T(8,128)(2,1)}, u32[]{:S(2)}) copy-start(bf16[32,4096]{1,0:T(8,128)(2,1)} %get-tuple-element.24) | copy-start | bytes 786436
  77.5 17.6 %copy-start.17 = (bf16[32,4096]{1,0:T(8,128)(2,1)S(1)}, bf16[32,4096]{1,0:T(8,128)(2,1)}, u32[]{:S(2)}) copy-start(bf16[32,4096]{1,0:T(8,128)(2,1)} %get-tuple-element.26) | copy-start | bytes 786436
  77.5 10.0 %collective-permute-start.18 = (bf16[64,2048]{1,0:T(8,128)(2,1)}, bf16[64,2048]{1,0:T(8,128)(2,1)S(1)}, u32[]{:S(2)}, u32[]{:S(2)}) collective-permute-start(bf16[64,2048]{1,0:T(8,128)(2,1)} %get-tuple-element.34), channel_id=1, source_target_pairs={{0,8},{8,0},{16,24},{24,16},{1,9},{9,1},{17,25},{25,17},{2,10},{10... | collective-permute-start | bytes 786440 | tf_op jit(solution)/shard_map/ppermute | solution.py:28
  78.0 34.6 %collective-permute-start.17 = (bf16[64,2048]{1,0:T(8,128)(2,1)}, bf16[64,2048]{1,0:T(8,128)(2,1)S(1)}, u32[]{:S(2)}, u32[]{:S(2)}) collective-permute-start(bf16[64,2048]{1,0:T(8,128)(2,1)} %get-tuple-element.32), channel_id=1, source_target_pairs={{0,8},{8,0},{16,24},{24,16},{1,9},{9,1},{17,25},{25,17},{2,10},{10... | collective-permute-start | bytes 786440 | tf_op jit(solution)/shard_map/ppermute | solution.py:28
  78.1 12.5 %collective-permute-start.4 = (bf16[32,4096]{1,0:T(8,128)(2,1)S(1)}, bf16[32,4096]{1,0:T(8,128)(2,1)S(1)}, u32[]{:S(2)}, u32[]{:S(2)}) collective-permute-start(bf16[32,4096]{1,0:T(8,128)(2,1)S(1)} %copy-done.20), channel_id=1, source_target_pairs={{0,1},{1,0},{2,3},{3,2},{4,5},{5,4},{6,7},{7,6},{8,9},{9,8},{10,11... | collective-permute-start | bytes 786440 | tf_op jit(solution)/shard_map/ppermute | solution.py:28
  79.6 14.8 %collective-permute-start.6 = (bf16[32,4096]{1,0:T(8,128)(2,1)S(1)}, bf16[32,4096]{1,0:T(8,128)(2,1)}, u32[]{:S(2)}, u32[]{:S(2)}) collective-permute-start(bf16[32,4096]{1,0:T(8,128)(2,1)S(1)} %copy-done.19), channel_id=1, source_target_pairs={{0,1},{1,0},{2,3},{3,2},{4,5},{5,4},{6,7},{7,6},{8,9},{9,8},{10,11... | collective-permute-start | bytes 786440 | tf_op jit(solution)/shard_map/ppermute | solution.py:28
  80.1 28.8 %collective-permute-start.8 = (bf16[32,4096]{1,0:T(8,128)(2,1)}, bf16[32,4096]{1,0:T(8,128)(2,1)S(1)}, u32[]{:S(2)}, u32[]{:S(2)}) collective-permute-start(bf16[32,4096]{1,0:T(8,128)(2,1)} %get-tuple-element.29), channel_id=1, source_target_pairs={{0,1},{1,0},{2,3},{3,2},{4,5},{5,4},{6,7},{7,6},{8,9},{9,8},{10,11... | collective-permute-start | bytes 786440 | tf_op jit(solution)/shard_map/ppermute | solution.py:28
  82.3 29.4 %copy-start.15 = (bf16[32,4096]{1,0:T(8,128)(2,1)S(1)}, bf16[32,4096]{1,0:T(8,128)(2,1)}, u32[]{:S(2)}) copy-start(bf16[32,4096]{1,0:T(8,128)(2,1)} %get-tuple-element.28) | copy-start | bytes 786436
  82.3 18.9 %all-to-all-start = ((f32[16,32,128]{2,1,0:T(8,128)}), f32[16,32,128]{2,1,0:T(8,128)S(1)}, u32[]{:S(2)}, u32[]{:S(2)}) async-start(f32[16,32,128]{2,1,0:T(8,128)} %bitcast.6), calls=%async_computation | async-start | bytes 524288 | tf_op jit(solution)/shard_map/all_to_all | solution.py:60
  87.5 42.5 %collective-permute-start.3 = (bf16[32,4096]{1,0:T(8,128)(2,1)}, bf16[32,4096]{1,0:T(8,128)(2,1)S(1)}, u32[]{:S(2)}, u32[]{:S(2)}) collective-permute-start(bf16[32,4096]{1,0:T(8,128)(2,1)} %get-tuple-element.23), channel_id=1, source_target_pairs={{0,1},{1,0},{2,3},{3,2},{4,5},{5,4},{6,7},{7,6},{8,9},{9,8},{10,11... | collective-permute-start | bytes 786440 | tf_op jit(solution)/shard_map/ppermute | solution.py:28
  89.5 24.5 %copy-start.16 = (bf16[64,2048]{1,0:T(8,128)(2,1)S(1)}, bf16[64,2048]{1,0:T(8,128)(2,1)}, u32[]{:S(2)}) copy-start(bf16[64,2048]{1,0:T(8,128)(2,1)} %get-tuple-element.31) | copy-start | bytes 786436
  90.5 23.5 %collective-permute-start.19 = (bf16[64,2048]{1,0:T(8,128)(2,1)S(1)}, bf16[64,2048]{1,0:T(8,128)(2,1)}, u32[]{:S(2)}, u32[]{:S(2)}) collective-permute-start(bf16[64,2048]{1,0:T(8,128)(2,1)S(1)} %add_convert_fusion), channel_id=1, source_target_pairs={{0,16},{8,24},{16,0},{24,8},{1,17},{9,25},{17,1},{25,9},{2,18},{10... | collective-permute-start | bytes 786440 | tf_op jit(solution)/shard_map/ppermute | solution.py:28
  94.4 35.6 %collective-permute-start.5 = (bf16[32,4096]{1,0:T(8,128)(2,1)S(1)}, bf16[32,4096]{1,0:T(8,128)(2,1)S(1)}, u32[]{:S(2)}, u32[]{:S(2)}) collective-permute-start(bf16[32,4096]{1,0:T(8,128)(2,1)S(1)} %add_convert_fusion.3), channel_id=1, source_target_pairs={{0,2},{1,3},{2,0},{3,1},{4,6},{5,7},{6,4},{7,5},{8,10},{9,11},{10,... | collective-permute-start | bytes 786440 | tf_op jit(solution)/shard_map/ppermute | solution.py:28
  102.1 27.9 %all-to-all-start.1 = ((f32[16,32,128]{2,1,0:T(8,128)}), f32[16,32,128]{2,1,0:T(8,128)S(1)}, u32[]{:S(2)}, u32[]{:S(2)}) async-start(f32[16,32,128]{2,1,0:T(8,128)} %broadcast_in_dim.3), calls=%async_computation.1 | async-start | bytes 524288 | tf_op jit(solution)/shard_map/all_to_all | solution.py:62
  108.9 26.0 %collective-permute-start.7 = (bf16[32,4096]{1,0:T(8,128)(2,1)S(1)}, bf16[32,4096]{1,0:T(8,128)(2,1)}, u32[]{:S(2)}, u32[]{:S(2)}) collective-permute-start(bf16[32,4096]{1,0:T(8,128)(2,1)S(1)} %add_convert_fusion.2), channel_id=1, source_target_pairs={{0,4},{1,5},{2,6},{3,7},{4,0},{5,1},{6,2},{7,3},{8,12},{9,13},{10,... | collective-permute-start | bytes 786440 | tf_op jit(solution)/shard_map/ppermute | solution.py:28
  112.5 22.4 %collective-permute-start.9 = (bf16[32,4096]{1,0:T(8,128)(2,1)}, bf16[32,4096]{1,0:T(8,128)(2,1)}, u32[]{:S(2)}, u32[]{:S(2)}) collective-permute-start(bf16[32,4096]{1,0:T(8,128)(2,1)} %add_convert_fusion.1), channel_id=1, source_target_pairs={{0,6},{1,7},{2,4},{3,5},{4,2},{5,3},{6,0},{7,1},{8,14},{9,15},{10,... | collective-permute-start | bytes 786440 | tf_op jit(solution)/shard_map/ppermute | solution.py:28
  115.1 19.9 %copy-start.2 = (bf16[32,4096]{1,0:T(8,128)(2,1)S(1)}, bf16[32,4096]{1,0:T(8,128)(2,1)}, u32[]{:S(2)}) copy-start(bf16[32,4096]{1,0:T(8,128)(2,1)} %get-tuple-element.22.refs_13_) | copy-start | bytes 786436
  129.9 7.1 %collective-permute-start.21 = (f32[512,128]{1,0:T(8,128)S(1)}, f32[512,128]{1,0:T(8,128)S(1)}, u32[]{:S(2)}, u32[]{:S(2)}) collective-permute-start(f32[512,128]{1,0:T(8,128)S(1)} %bitcast.24), channel_id=1, source_target_pairs={{0,8},{8,0},{1,9},{9,1},{2,10},{10,2},{3,11},{11,3},{4,12},{12,4},... | collective-permute-start | bytes 786440 | tf_op jit(solution)/shard_map/ppermute | solution.py:28

commit v3 on v2

--- a/solution.py
+++ b/solution.py
@@ -206,14 +206,16 @@
     )(own, *pieces, in_hbm(expanded), after)
 
 
-def weight_product(own, lefts, rights, turned, channels, after):
-    cols, rows, pair_width = turned.shape
+def weight_product(own, lefts, rights, turned, channels, after, blocks, earlier=()):
+    first, count = blocks
+    _, rows, pair_width = turned.shape
     width = lefts[0].shape[1]
     sequences = lefts[0].shape[0] * len(lefts)
 
     def kernel(own_ref, *refs):
         left_refs, right_refs = refs[: len(lefts)], refs[len(lefts) : len(lefts) + len(rights)]
-        turned_ref, _, out_ref, left, right, right_t, outer = refs[len(lefts) + len(rights) :]
+        turned_ref, _, *earlier_refs = refs[len(lefts) + len(rights) : -5]
+        out_ref, left, right, right_t, outer = refs[-5:]
         step = pl.program_id(0)
 
         @pl.when(step == 0)
@@ -237,7 +239,7 @@
 
         @pl.when(step == 0)
         def _():
-            out_ref[...] = total
+            out_ref[...] = total + earlier_refs[0][...] if earlier else total
 
         @pl.when(step != 0)
         def _():
@@ -246,11 +248,12 @@
     block = BLOCK * channels
     return pl.pallas_call(
         kernel,
-        grid=(cols // BLOCK,),
+        grid=(count,),
         in_specs=[pl.BlockSpec(memory_space=pltpu.SMEM)]
         + [whole_spec(piece) for piece in lefts]
-        + [pl.BlockSpec((piece.shape[0], block), lambda b: (0, b)) for piece in rights]
-        + [pl.BlockSpec((BLOCK, rows, pair_width), lambda b: (b, 0, 0)), pl.BlockSpec(memory_space=pl.ANY)],
+        + [pl.BlockSpec((piece.shape[0], block), lambda b: (0, first + b)) for piece in rights]
+        + [pl.BlockSpec((BLOCK, rows, pair_width), lambda b: (first + b, 0, 0)), pl.BlockSpec(memory_space=pl.ANY)]
+        + [whole_spec(array) for array in earlier],
         out_specs=pl.BlockSpec((channels * channels, pair_width), lambda b: (0, 0)),
         out_shape=jax.ShapeDtypeStruct((channels * channels, pair_width), F32),
         scratch_shapes=[
@@ -260,9 +263,9 @@
             pltpu.VMEM((channels * channels, BLOCK * rows), BF16),
         ],
         compiler_params=params(18),
-        cost_estimate=cost(4 * sequences * cols * channels * width, 2 * sequences * width),
+        cost_estimate=cost(6 * sequences * count * BLOCK * channels * width, 2 * sequences * width),
         name="weight",
-    )(own, *lefts, *rights, turned, after)
+    )(own, *lefts, *rights, turned, after, *earlier)
 
 
 def by_tiles(left_panel, right_panel, pair_grad, out_weight):
@@ -290,7 +293,12 @@
         arrays = expand(pair_grad, out_weight, channels, (0, early))
     expanded, turned = expand(pair_grad, out_weight, channels, (early, blocks - early), arrays)
     left_slots = left_product(own, rights, expanded, len(lefts))
-    weight_terms = weight_product(own, lefts, rights, turned, channels, left_slots[0])
+    weight_terms, after = (), left_slots[0]
+    for part in ((0, early), (early, blocks - early)):
+        if part[1]:
+            after = weight_product(own, lefts, rights, turned, channels, after, part, weight_terms)
+            weight_terms = (after,)
+    weight_terms = after
     right_slots = right_product(own[::-1], lefts, expanded, len(rights), weight_terms)
 
     left_grad = scatter(left_slots, "col") * scale

time: 140 us -> 142 us (1.014)
  Pallas kernels: 48.2 us -> 50.2 us
    pallas_call x1 -> x2, Pallas kernels: 12.4 us -> 14.3 us  [weight_product(): pl.pallas_call(kernel, grid=(count,), in_specs=[pl.BlockSpec(memory_space...]
where the time goes in v3:
time: 142 us; the launch traced here: 140 us
  Pallas kernels  50.2 us (35%)
  starting transfers between devices  36.3 us (26%)
  waiting for transfers between devices  35.6 us (25%)
  local copies, waits for them, and re-layouts  9.88 us (7%)
  other arithmetic  6.85 us (5%)
    ppermute x22, starting transfers between devices, permute(): return lax.ppermute(array, axis, toggled(axis, bit))  24.4 us
    ppermute x22, waiting for transfers between devices, permute(): return lax.ppermute(array, axis, toggled(axis, bit))  17.9 us
    pallas_call x2, Pallas kernels, expand(): pl.pallas_call(kernel, grid=(count,), in_specs=[pl.BlockSpec((rows, BLOCK...  15.7 us
    pallas_call x2, Pallas kernels, weight_product(): pl.pallas_call(kernel, grid=(count,), in_specs=[pl.BlockSpec(memory_space...  14.3 us
    all_to_all x1, waiting for transfers between devices, reduce_everywhere(): lax.all_to_all(jnp.broadcast_to(part, (count, *part.shape)), chips, 0, 0,...  12.5 us
    pallas_call x1, Pallas kernels, right_product(): pl.pallas_call(kernel, grid=(depth // tile,), in_specs=[pl.BlockSpec(memo...  10.1 us
    pallas_call x1, Pallas kernels, left_product(): pl.pallas_call(kernel, grid=(width // tile,), in_specs=[pl.BlockSpec(memo...  10.1 us
    unnamed x46, local copies, waits for them, and re-layouts  8.5 us
  transfers between devices with their start and end apart: 24, of which 7 were waited for; matrix products, arithmetic and copies ran while one was open for 8% of the time, Pallas kernels for 26%

profile of v3, /device:TPU:0, one launch (start us, length us, event | category | flops | bytes accessed | tf_op | source)
XLA Modules:
  0.0 139.8 jit_solution(16950191521121730664)
XLA Ops:
  0.6 2.1 %copy.11 = bf16[64,64,32]{0,2,1:T(8,128)(2,1)S(1)} copy(bf16[64,64,32]{1,2,0:T(8,128)(2,1)} %param.5) | data formatting | bytes 524288 | tf_op args[1]
  2.8 0.2 copy.14.refs_0_.refs_8_
  3.0 0.0 copy-start.3
  3.0 3.1 %collective-permute-start.1 = (bf16[64,2048]{1,0:T(8,128)(2,1)S(1)}, bf16[64,2048]{1,0:T(8,128)(2,1)S(1)}, u32[]{:S(2)}, u32[]{:S(2)}) collective-permute-start(bf16[64,2048]{1,0:T(8,128)(2,1)S(1)} %copy.14.refs_0_.refs_8_), channel_id=1, source_target_pairs={{0,16},{8,24},{16,0},{24,8},{1,17},{9,25},{17,1},{25,9},{2,18},{10... | collective-permute-start | bytes 786440 | tf_op jit(solution)/shard_map/ppermute | solution.py:28
  6.0 1.1 copy.22
  7.1 1.6 %collective-permute-start.11 = (bf16[32,4096]{1,0:T(8,128)(2,1)S(1)}, bf16[32,4096]{1,0:T(8,128)(2,1)S(1)}, u32[]{:S(2)}, u32[]{:S(2)}) collective-permute-start(bf16[32,4096]{1,0:T(8,128)(2,1)S(1)} %bitcast.18), channel_id=1, source_target_pairs={{0,2},{1,3},{2,0},{3,1},{4,6},{5,7},{6,4},{7,5},{8,10},{9,11},{10,... | collective-permute-start | bytes 786440 | tf_op jit(solution)/shard_map/ppermute | solution.py:28
  8.8 2.6 %collective-permute-start.13 = (bf16[32,4096]{1,0:T(8,128)(2,1)S(1)}, bf16[32,4096]{1,0:T(8,128)(2,1)S(1)}, u32[]{:S(2)}, u32[]{:S(2)}) collective-permute-start(bf16[32,4096]{1,0:T(8,128)(2,1)S(1)} %bitcast.19), channel_id=1, source_target_pairs={{0,4},{1,5},{2,6},{3,7},{4,0},{5,1},{6,2},{7,3},{8,12},{9,13},{10,... | collective-permute-start | bytes 786440 | tf_op jit(solution)/shard_map/ppermute | solution.py:28
  11.3 0.2 collective-permute-start.15
  11.6 7.9 %expand.2 = (bf16[2048,4096]{1,0:T(8,128)(2,1)}, bf16[64,128,128]{2,1,0:T(8,128)(2,1)}) custom-call(bf16[128,64,128]{2,1,0:T(8,128)(2,1)} %refs_0_.3, bf16[1024,128]{1,0:T(8,128)(2,1)} %refs_1_.3), custom_call_target="tpu_custom_call" | custom-call | flops 2147483648 | bytes 8388608 | tf_op jit(solution)/shard_map/expand/pallas_call | solution.py:97
  19.5 0.0 collective-permute-done.1.refs_2_.refs_10_
  19.5 0.0 copy-start.8
  19.5 0.1 collective-permute-start.2
  19.6 0.1 pad_add_fusion.own_ref
  19.7 0.1 rev.3.own_ref
  19.8 7.8 %expand.3 = (bf16[2048,4096]{1,0:T(8,128)(2,1)}, bf16[64,128,128]{2,1,0:T(8,128)(2,1)}) custom-call(bf16[128,64,128]{2,1,0:T(8,128)(2,1)} %refs_0_.3, bf16[1024,128]{1,0:T(8,128)(2,1)} %refs_1_.3, bf16[2048,4096]{1,0:T(8,128)(2,1)} %get-tuple-element.19.refs_2_, ...), custom_call_target="tpu_custom_call", output_to_operand_aliasing={{0}: (2, {}), {1}: (3, {})} | custom-call | flops 2147483648 | bytes 8388608 | tf_op jit(solution)/shard_map/expand/pallas_call | solution.py:97
  27.6 0.0 copy-start.9
  27.6 1.6 %collective-permute-start.10 = (bf16[32,4096]{1,0:T(8,128)(2,1)S(1)}, bf16[32,4096]{1,0:T(8,128)(2,1)S(1)}, u32[]{:S(2)}, u32[]{:S(2)}) collective-permute-start(bf16[32,4096]{1,0:T(8,128)(2,1)S(1)} %bitcast.21), channel_id=1, source_target_pairs={{0,1},{1,0},{2,3},{3,2},{4,5},{5,4},{6,7},{7,6},{8,9},{9,8},{10,11... | collective-permute-start | bytes 786440 | tf_op jit(solution)/shard_map/ppermute | solution.py:28
  29.2 0.5 collective-permute-start.12
  29.7 0.4 collective-permute-done.13.refs_4_
  30.1 1.5 %collective-permute-start.14 = (bf16[32,4096]{1,0:T(8,128)(2,1)S(1)}, bf16[32,4096]{1,0:T(8,128)(2,1)S(1)}, u32[]{:S(2)}, u32[]{:S(2)}) collective-permute-start(bf16[32,4096]{1,0:T(8,128)(2,1)S(1)} %collective-permute-done.13.refs_4_), channel_id=1, source_target_pairs={{0,1},{1,0},{2,3},{3,2},{4,5},{5,4},{6,7},{7,6},{8,9},{9,8},{10,11... | collective-permute-start | bytes 786440 | tf_op jit(solution)/shard_map/ppermute | solution.py:28
  31.6 0.0 collective-permute-done.15.refs_6_
  31.6 0.5 collective-permute-start.16
  32.2 0.7 copy-done.10
  32.9 10.1 %left.1 = (bf16[32,4096]{1,0:T(8,128)(2,1)}, bf16[32,4096]{1,0:T(8,128)(2,1)}, bf16[32,4096]{1,0:T(8,128)(2,1)}, bf16[32,4096]{1,0:T(8,128)(2,1)}, bf16[32,4096]...) custom-call(s32[2]{0:T(128)S(1)} %pad_add_fusion.own_ref, ...), custom_call_target="tpu_custom_call" | custom-call | flops 4294967296 | bytes 16777216 | tf_op jit(solution)/shard_map/left/pallas_call | solution.py:159
  43.0 0.0 collective-permute-done.12.refs_3_
  43.0 5.1 %collective-permute-done.14.refs_5_ = bf16[32,4096]{1,0:T(8,128)(2,1)S(1)} collective-permute-done((bf16[32,4096]{1,0:T(8,128)(2,1)S(1)}, bf16[32,4096]{1,0:T(8,128)(2,1)S(1)}, u32[]{:S(2)}, u32[]{:S(2)}) %collective-permute-start.14) | collective-permute-done | bytes 262176 | tf_op jit(solution)/shard_map/ppermute | solution.py:28
  48.1 5.1 %collective-permute-done.16.refs_7_ = bf16[32,4096]{1,0:T(8,128)(2,1)S(1)} collective-permute-done((bf16[32,4096]{1,0:T(8,128)(2,1)S(1)}, bf16[32,4096]{1,0:T(8,128)(2,1)S(1)}, u32[]{:S(2)}, u32[]{:S(2)}) %collective-permute-start.16) | collective-permute-done | bytes 262176 | tf_op jit(solution)/shard_map/ppermute | solution.py:28
  53.2 0.7 copy-done.14
  53.9 0.9 copy-done.1
  54.9 7.1 %weight.2.refs_13_.refs_14_ = f32[1024,128]{1,0:T(8,128)S(1)} custom-call(s32[2]{0:T(128)S(1)} %pad_add_fusion.own_ref, bf16[32,4096]{1,0:T(8,128)(2,1)} %bitcast.22, bf16[32,4096]{1,0:T(8,128)(2,1)} %copy-done.11, bf16[32,4096]{1,0:T(8,128)(2,1)} %copy-done.5, bf16[32,4096]{1,0:T(8,128)(2,1)} %copy-done.12, bf16[32,4096]{1,0:T(8,128)(2,1)} %copy-done.6, ...), custom_call_target="tpu_custom_call" | custom-call | flops 6442450944 | bytes 2097152 | tf_op jit(solution)/shard_map/weight/pallas_call | solution.py:249
  62.0 7.2 %weight.3.refs_9_ = f32[1024,128]{1,0:T(8,128)S(1)} custom-call(s32[2]{0:T(128)S(1)} %pad_add_fusion.own_ref, bf16[32,4096]{1,0:T(8,128)(2,1)} %bitcast.23, bf16[32,4096]{1,0:T(8,128)(2,1)} %copy-done.11, bf16[32,4096]{1,0:T(8,128)(2,1)} %copy-done.5, bf16[32,4096]{1,0:T(8,128)(2,1)} %copy-done.12, bf16[32,4096]{1,0:T(8,128)(2,1)} %copy-done.6, ...), custom_call_target="tpu_custom_call" | custom-call | flops 6442450944 | bytes 2097152 | tf_op jit(solution)/shard_map/weight/pallas_call | solution.py:249
  69.3 0.1 collective-permute-start.20
  69.3 10.1 %right.1 = (bf16[64,2048]{1,0:T(8,128)(2,1)}, bf16[64,2048]{1,0:T(8,128)(2,1)}, bf16[64,2048]{1,0:T(8,128)(2,1)}, bf16[64,2048]{1,0:T(8,128)(2,1)}) custom-call(s32[2]{0:T(128)S(1)} %rev.3.own_ref, bf16[32,4096]{1,0:T(8,128)(2,1)} %bitcast.24, bf16[32,4096]{1,0:T(8,128)(2,1)} %copy-done.11, bf16[32,4096]{1,0:T(8,128)(2,1)} %copy-done.5, ...), custom_call_target="tpu_custom_call" | custom-call | flops 4294967296 | bytes 16777216 | tf_op jit(solution)/shard_map/right/pallas_call | solution.py:194
  79.4 0.5 collective-permute-start.18
  79.9 0.1 collective-permute-start.17
  80.0 1.5 %collective-permute-start.4 = (bf16[32,4096]{1,0:T(8,128)(2,1)S(1)}, bf16[32,4096]{1,0:T(8,128)(2,1)S(1)}, u32[]{:S(2)}, u32[]{:S(2)}) collective-permute-start(bf16[32,4096]{1,0:T(8,128)(2,1)S(1)} %copy-done.20), channel_id=1, source_target_pairs={{0,1},{1,0},{2,3},{3,2},{4,5},{5,4},{6,7},{7,6},{8,9},{9,8},{10,11... | collective-permute-start | bytes 786440 | tf_op jit(solution)/shard_map/ppermute | solution.py:28
  81.5 0.5 collective-permute-start.6
  82.0 1.5 %collective-permute-start.8 = (bf16[32,4096]{1,0:T(8,128)(2,1)}, bf16[32,4096]{1,0:T(8,128)(2,1)S(1)}, u32[]{:S(2)}, u32[]{:S(2)}) collective-permute-start(bf16[32,4096]{1,0:T(8,128)(2,1)} %get-tuple-element.29), channel_id=1, source_target_pairs={{0,1},{1,0},{2,3},{3,2},{4,5},{5,4},{6,7},{7,6},{8,9},{9,8},{10,11... | collective-permute-start | bytes 786440 | tf_op jit(solution)/shard_map/ppermute | solution.py:28
  83.5 0.8 dynamic-slice_add_fusion
  84.3 5.1 %all-to-all-start = ((f32[16,32,128]{2,1,0:T(8,128)}), f32[16,32,128]{2,1,0:T(8,128)S(1)}, u32[]{:S(2)}, u32[]{:S(2)}) async-start(f32[16,32,128]{2,1,0:T(8,128)} %bitcast.6), calls=%async_computation | async-start | bytes 524288 | tf_op jit(solution)/shard_map/all_to_all | solution.py:60
  89.4 0.0 collective-permute-done.18
  89.4 2.0 %collective-permute-start.3 = (bf16[32,4096]{1,0:T(8,128)(2,1)}, bf16[32,4096]{1,0:T(8,128)(2,1)S(1)}, u32[]{:S(2)}, u32[]{:S(2)}) collective-permute-start(bf16[32,4096]{1,0:T(8,128)(2,1)} %get-tuple-element.23), channel_id=1, source_target_pairs={{0,1},{1,0},{2,3},{3,2},{4,5},{5,4},{6,7},{7,6},{8,9},{9,8},{10,11... | collective-permute-start | bytes 786440 | tf_op jit(solution)/shard_map/ppermute | solution.py:28
  91.4 1.1 add_convert_fusion
  92.5 0.0 collective-permute-done.4
  92.5 1.5 %collective-permute-start.19 = (bf16[64,2048]{1,0:T(8,128)(2,1)S(1)}, bf16[64,2048]{1,0:T(8,128)(2,1)}, u32[]{:S(2)}, u32[]{:S(2)}) collective-permute-start(bf16[64,2048]{1,0:T(8,128)(2,1)S(1)} %add_convert_fusion), channel_id=1, source_target_pairs={{0,16},{8,24},{16,0},{24,8},{1,17},{9,25},{17,1},{25,9},{2,18},{10... | collective-permute-start | bytes 786440 | tf_op jit(solution)/shard_map/ppermute | solution.py:28
  94.0 0.1 add_convert_fusion.3
  94.1 2.2 %collective-permute-done.6 = bf16[32,4096]{1,0:T(8,128)(2,1)} collective-permute-done((bf16[32,4096]{1,0:T(8,128)(2,1)S(1)}, bf16[32,4096]{1,0:T(8,128)(2,1)}, u32[]{:S(2)}, u32[]{:S(2)}) %collective-permute-start.6) | collective-permute-done | bytes 262176 | tf_op jit(solution)/shard_map/ppermute | solution.py:28
  96.3 0.7 collective-permute-start.5
  97.0 1.0 add_convert_fusion.2
  98.0 5.2 %all-to-all-done = f32[16,32,128]{2,1,0:T(8,128)S(1)} async-done(((f32[16,32,128]{2,1,0:T(8,128)}), f32[16,32,128]{2,1,0:T(8,128)S(1)}, u32[]{:S(2)}, u32[]{:S(2)}) %all-to-all-start) | async-done | bytes 262176 | tf_op jit(solution)/shard_map/all_to_all | solution.py:60
  103.3 0.7 broadcast_in_dim.3
  104.0 6.8 %all-to-all-start.1 = ((f32[16,32,128]{2,1,0:T(8,128)}), f32[16,32,128]{2,1,0:T(8,128)S(1)}, u32[]{:S(2)}, u32[]{:S(2)}) async-start(f32[16,32,128]{2,1,0:T(8,128)} %broadcast_in_dim.3), calls=%async_computation.1 | async-start | bytes 524288 | tf_op jit(solution)/shard_map/all_to_all | solution.py:62
  110.8 0.0 collective-permute-done.8
  110.8 2.9 %collective-permute-start.7 = (bf16[32,4096]{1,0:T(8,128)(2,1)S(1)}, bf16[32,4096]{1,0:T(8,128)(2,1)}, u32[]{:S(2)}, u32[]{:S(2)}) collective-permute-start(bf16[32,4096]{1,0:T(8,128)(2,1)S(1)} %add_convert_fusion.2), channel_id=1, source_target_pairs={{0,4},{1,5},{2,6},{3,7},{4,0},{5,1},{6,2},{7,3},{8,12},{9,13},{10,... | collective-permute-start | bytes 786440 | tf_op jit(solution)/shard_map/ppermute | solution.py:28
  113.7 0.8 add_convert_fusion.1
  114.5 1.5 %collective-permute-start.9 = (bf16[32,4096]{1,0:T(8,128)(2,1)}, bf16[32,4096]{1,0:T(8,128)(2,1)}, u32[]{:S(2)}, u32[]{:S(2)}) collective-permute-start(bf16[32,4096]{1,0:T(8,128)(2,1)} %add_convert_fusion.1), channel_id=1, source_target_pairs={{0,6},{1,7},{2,4},{3,5},{4,2},{5,3},{6,0},{7,1},{8,14},{9,15},{10,... | collective-permute-start | bytes 786440 | tf_op jit(solution)/shard_map/ppermute | solution.py:28
  115.9 1.1 add_multiply_fusion
  117.0 0.3 copy.17
  117.4 2.0 %copy.18 = f32[64,64,32]{1,2,0:T(8,128)} copy(f32[64,64,32]{0,2,1:T(8,128)S(1)} %bitcast.16) | data formatting | bytes 1048576
  119.3 12.5 %all-to-all-done.1 = f32[16,32,128]{2,1,0:T(8,128)S(1)} async-done(((f32[16,32,128]{2,1,0:T(8,128)}), f32[16,32,128]{2,1,0:T(8,128)S(1)}, u32[]{:S(2)}, u32[]{:S(2)}) %all-to-all-start.1) | async-done | bytes 262176 | tf_op jit(solution)/shard_map/all_to_all | solution.py:62
  131.9 5.0 %collective-permute-done.7 = bf16[32,4096]{1,0:T(8,128)(2,1)} collective-permute-done((bf16[32,4096]{1,0:T(8,128)(2,1)S(1)}, bf16[32,4096]{1,0:T(8,128)(2,1)}, u32[]{:S(2)}, u32[]{:S(2)}) %collective-permute-start.7) | collective-permute-done | bytes 262176 | tf_op jit(solution)/shard_map/ppermute | solution.py:28
  136.9 1.2 multiply_bitcast_fusion
  138.1 0.9 copy.19
  139.0 0.8 maximum_select_fusion
  (52 shorter events, 0.2 us)
Async XLA Ops:
  3.0 16.5 %copy-start.3 = (bf16[64,2048]{1,0:T(8,128)(2,1)}, bf16[64,2048]{1,0:T(8,128)(2,1)S(1)}, u32[]{:S(2)}) copy-start(bf16[64,2048]{1,0:T(8,128)(2,1)S(1)} %copy.14.refs_0_.refs_8_) | copy-start | bytes 786436
  3.0 16.5 %collective-permute-start.1 = (bf16[64,2048]{1,0:T(8,128)(2,1)S(1)}, bf16[64,2048]{1,0:T(8,128)(2,1)S(1)}, u32[]{:S(2)}, u32[]{:S(2)}) collective-permute-start(bf16[64,2048]{1,0:T(8,128)(2,1)S(1)} %copy.14.refs_0_.refs_8_), channel_id=1, source_target_pairs={{0,16},{8,24},{16,0},{24,8},{1,17},{9,25},{17,1},{25,9},{2,18},{10... | collective-permute-start | bytes 786440 | tf_op jit(solution)/shard_map/ppermute | solution.py:28
  6.0 21.5 %collective-permute-start = (bf16[64,2048]{1,0:T(8,128)(2,1)S(1)}, bf16[64,2048]{1,0:T(8,128)(2,1)S(1)}, u32[]{:S(2)}, u32[]{:S(2)}) collective-permute-start(bf16[64,2048]{1,0:T(8,128)(2,1)S(1)} %copy.14.refs_0_.refs_8_), channel_id=1, source_target_pairs={{0,8},{8,0},{16,24},{24,16},{1,9},{9,1},{17,25},{25,17},{2,10},{10... | collective-permute-start | bytes 786440 | tf_op jit(solution)/shard_map/ppermute | solution.py:28
  7.1 20.5 %copy-start.4 = (bf16[4,8,32,128]{3,1,2,0:T(8,128)(2,1)}, bf16[4,8,32,128]{3,1,2,0:T(8,128)(2,1)S(1)}, u32[]{:S(2)}) copy-start(bf16[4,8,32,128]{3,1,2,0:T(8,128)(2,1)S(1)} %copy.22) | copy-start | bytes 786436
  7.1 22.0 %collective-permute-start.11 = (bf16[32,4096]{1,0:T(8,128)(2,1)S(1)}, bf16[32,4096]{1,0:T(8,128)(2,1)S(1)}, u32[]{:S(2)}, u32[]{:S(2)}) collective-permute-start(bf16[32,4096]{1,0:T(8,128)(2,1)S(1)} %bitcast.18), channel_id=1, source_target_pairs={{0,2},{1,3},{2,0},{3,1},{4,6},{5,7},{6,4},{7,5},{8,10},{9,11},{10,... | collective-permute-start | bytes 786440 | tf_op jit(solution)/shard_map/ppermute | solution.py:28
  8.8 21.4 %collective-permute-start.13 = (bf16[32,4096]{1,0:T(8,128)(2,1)S(1)}, bf16[32,4096]{1,0:T(8,128)(2,1)S(1)}, u32[]{:S(2)}, u32[]{:S(2)}) collective-permute-start(bf16[32,4096]{1,0:T(8,128)(2,1)S(1)} %bitcast.19), channel_id=1, source_target_pairs={{0,4},{1,5},{2,6},{3,7},{4,0},{5,1},{6,2},{7,3},{8,12},{9,13},{10,... | collective-permute-start | bytes 786440 | tf_op jit(solution)/shard_map/ppermute | solution.py:28
  11.3 20.3 %collective-permute-start.15 = (bf16[32,4096]{1,0:T(8,128)(2,1)S(1)}, bf16[32,4096]{1,0:T(8,128)(2,1)S(1)}, u32[]{:S(2)}, u32[]{:S(2)}) collective-permute-start(bf16[32,4096]{1,0:T(8,128)(2,1)S(1)} %bitcast.20), channel_id=1, source_target_pairs={{0,6},{1,7},{2,4},{3,5},{4,2},{5,3},{6,0},{7,1},{8,14},{9,15},{10,... | collective-permute-start | bytes 786440 | tf_op jit(solution)/shard_map/ppermute | solution.py:28
  19.5 8.1 %copy-start.8 = (bf16[64,2048]{1,0:T(8,128)(2,1)}, bf16[64,2048]{1,0:T(8,128)(2,1)S(1)}, u32[]{:S(2)}) copy-start(bf16[64,2048]{1,0:T(8,128)(2,1)S(1)} %collective-permute-done.1.refs_2_.refs_10_) | copy-start | bytes 786436
  19.5 12.7 %collective-permute-start.2 = (bf16[64,2048]{1,0:T(8,128)(2,1)S(1)}, bf16[64,2048]{1,0:T(8,128)(2,1)S(1)}, u32[]{:S(2)}, u32[]{:S(2)}) collective-permute-start(bf16[64,2048]{1,0:T(8,128)(2,1)S(1)} %collective-permute-done.1.refs_2_.refs_10_), channel_id=1, source_target_pairs={{0,8},{8,0},{16,24},{24,16},{1,9},{9,1},{17,25},{25,17},{2,10},{10... | collective-permute-start | bytes 786440 | tf_op jit(solution)/shard_map/ppermute | solution.py:28
  27.6 4.6 %copy-start.9 = (bf16[64,2048]{1,0:T(8,128)(2,1)}, bf16[64,2048]{1,0:T(8,128)(2,1)S(1)}, u32[]{:S(2)}) copy-start(bf16[64,2048]{1,0:T(8,128)(2,1)S(1)} %collective-permute-done.refs_1_.refs_9_) | copy-start | bytes 786436
  27.6 15.4 %collective-permute-start.10 = (bf16[32,4096]{1,0:T(8,128)(2,1)S(1)}, bf16[32,4096]{1,0:T(8,128)(2,1)S(1)}, u32[]{:S(2)}, u32[]{:S(2)}) collective-permute-start(bf16[32,4096]{1,0:T(8,128)(2,1)S(1)} %bitcast.21), channel_id=1, source_target_pairs={{0,1},{1,0},{2,3},{3,2},{4,5},{5,4},{6,7},{7,6},{8,9},{9,8},{10,11... | collective-permute-start | bytes 786440 | tf_op jit(solution)/shard_map/ppermute | solution.py:28
  29.2 13.8 %copy-start.5 = (bf16[32,4096]{1,0:T(8,128)(2,1)}, bf16[32,4096]{1,0:T(8,128)(2,1)S(1)}, u32[]{:S(2)}) copy-start(bf16[32,4096]{1,0:T(8,128)(2,1)S(1)} %collective-permute-done.11.refs_2_) | copy-start | bytes 786436
  29.2 13.8 %collective-permute-start.12 = (bf16[32,4096]{1,0:T(8,128)(2,1)S(1)}, bf16[32,4096]{1,0:T(8,128)(2,1)S(1)}, u32[]{:S(2)}, u32[]{:S(2)}) collective-permute-start(bf16[32,4096]{1,0:T(8,128)(2,1)S(1)} %collective-permute-done.11.refs_2_), channel_id=1, source_target_pairs={{0,1},{1,0},{2,3},{3,2},{4,5},{5,4},{6,7},{7,6},{8,9},{9,8},{10,11... | collective-permute-start | bytes 786440 | tf_op jit(solution)/shard_map/ppermute | solution.py:28
  30.1 12.8 %copy-start.6 = (bf16[32,4096]{1,0:T(8,128)(2,1)}, bf16[32,4096]{1,0:T(8,128)(2,1)S(1)}, u32[]{:S(2)}) copy-start(bf16[32,4096]{1,0:T(8,128)(2,1)S(1)} %collective-permute-done.13.refs_4_) | copy-start | bytes 786436
  30.1 18.0 %collective-permute-start.14 = (bf16[32,4096]{1,0:T(8,128)(2,1)S(1)}, bf16[32,4096]{1,0:T(8,128)(2,1)S(1)}, u32[]{:S(2)}, u32[]{:S(2)}) collective-permute-start(bf16[32,4096]{1,0:T(8,128)(2,1)S(1)} %collective-permute-done.13.refs_4_), channel_id=1, source_target_pairs={{0,1},{1,0},{2,3},{3,2},{4,5},{5,4},{6,7},{7,6},{8,9},{9,8},{10,11... | collective-permute-start | bytes 786440 | tf_op jit(solution)/shard_map/ppermute | solution.py:28
  31.6 11.3 %copy-start.7 = (bf16[32,4096]{1,0:T(8,128)(2,1)}, bf16[32,4096]{1,0:T(8,128)(2,1)S(1)}, u32[]{:S(2)}) copy-start(bf16[32,4096]{1,0:T(8,128)(2,1)S(1)} %collective-permute-done.15.refs_6_) | copy-start | bytes 786436
  31.6 21.6 %collective-permute-start.16 = (bf16[32,4096]{1,0:T(8,128)(2,1)S(1)}, bf16[32,4096]{1,0:T(8,128)(2,1)S(1)}, u32[]{:S(2)}, u32[]{:S(2)}) collective-permute-start(bf16[32,4096]{1,0:T(8,128)(2,1)S(1)} %collective-permute-done.15.refs_6_), channel_id=1, source_target_pairs={{0,1},{1,0},{2,3},{3,2},{4,5},{5,4},{6,7},{7,6},{8,9},{9,8},{10,11... | collective-permute-start | bytes 786440 | tf_op jit(solution)/shard_map/ppermute | solution.py:28
  32.2 0.7 copy-start.10
  32.9 21.1 %copy-start = (bf16[64,128,128]{2,1,0:T(8,128)(2,1)S(1)}, bf16[64,128,128]{2,1,0:T(8,128)(2,1)}, u32[]{:S(2)}) copy-start(bf16[64,128,128]{2,1,0:T(8,128)(2,1)} %get-tuple-element.30.refs_12_) | copy-start | bytes 6291460
  43.0 10.2 %copy-start.11 = (bf16[32,4096]{1,0:T(8,128)(2,1)}, bf16[32,4096]{1,0:T(8,128)(2,1)S(1)}, u32[]{:S(2)}) copy-start(bf16[32,4096]{1,0:T(8,128)(2,1)S(1)} %collective-permute-done.10.refs_1_) | copy-start | bytes 786436
  43.0 10.2 %copy-start.12 = (bf16[32,4096]{1,0:T(8,128)(2,1)}, bf16[32,4096]{1,0:T(8,128)(2,1)S(1)}, u32[]{:S(2)}) copy-start(bf16[32,4096]{1,0:T(8,128)(2,1)S(1)} %collective-permute-done.12.refs_3_) | copy-start | bytes 786436
  48.1 5.2 %copy-start.13 = (bf16[32,4096]{1,0:T(8,128)(2,1)}, bf16[32,4096]{1,0:T(8,128)(2,1)S(1)}, u32[]{:S(2)}) copy-start(bf16[32,4096]{1,0:T(8,128)(2,1)S(1)} %collective-permute-done.14.refs_5_) | copy-start | bytes 786436
  53.2 0.7 copy-start.14
  53.9 1.0 copy-start.1
  69.2 10.8 %copy-start.20 = (bf16[32,4096]{1,0:T(8,128)(2,1)S(1)}, bf16[32,4096]{1,0:T(8,128)(2,1)}, u32[]{:S(2)}) copy-start(bf16[32,4096]{1,0:T(8,128)(2,1)} %get-tuple-element.25) | copy-start | bytes 786436
  69.2 12.3 %copy-start.19 = (bf16[32,4096]{1,0:T(8,128)(2,1)S(1)}, bf16[32,4096]{1,0:T(8,128)(2,1)}, u32[]{:S(2)}) copy-start(bf16[32,4096]{1,0:T(8,128)(2,1)} %get-tuple-element.27) | copy-start | bytes 786436
  69.3 12.8 %collective-permute-start.20 = (f32[512,128]{1,0:T(8,128)S(1)}, f32[512,128]{1,0:T(8,128)S(1)}, u32[]{:S(2)}, u32[]{:S(2)}) collective-permute-start(f32[512,128]{1,0:T(8,128)S(1)} %constant_dynamic-slice_fusion), channel_id=1, source_target_pairs={{0,8},{8,0},{1,9},{9,1},{2,10},{10,2},{3,11},{11,3},{4,12},{12,4},... | collective-permute-start | bytes 786440 | tf_op jit(solution)/shard_map/ppermute | solution.py:28
  79.4 14.6 %copy-start.18 = (bf16[32,4096]{1,0:T(8,128)(2,1)S(1)}, bf16[32,4096]{1,0:T(8,128)(2,1)}, u32[]{:S(2)}) copy-start(bf16[32,4096]{1,0:T(8,128)(2,1)} %get-tuple-element.24) | copy-start | bytes 786436
  79.4 17.6 %copy-start.17 = (bf16[32,4096]{1,0:T(8,128)(2,1)S(1)}, bf16[32,4096]{1,0:T(8,128)(2,1)}, u32[]{:S(2)}) copy-start(bf16[32,4096]{1,0:T(8,128)(2,1)} %get-tuple-element.26) | copy-start | bytes 786436
  79.4 10.0 %collective-permute-start.18 = (bf16[64,2048]{1,0:T(8,128)(2,1)}, bf16[64,2048]{1,0:T(8,128)(2,1)S(1)}, u32[]{:S(2)}, u32[]{:S(2)}) collective-permute-start(bf16[64,2048]{1,0:T(8,128)(2,1)} %get-tuple-element.34), channel_id=1, source_target_pairs={{0,8},{8,0},{16,24},{24,16},{1,9},{9,1},{17,25},{25,17},{2,10},{10... | collective-permute-start | bytes 786440 | tf_op jit(solution)/shard_map/ppermute | solution.py:28
  79.9 34.6 %collective-permute-start.17 = (bf16[64,2048]{1,0:T(8,128)(2,1)}, bf16[64,2048]{1,0:T(8,128)(2,1)S(1)}, u32[]{:S(2)}, u32[]{:S(2)}) collective-permute-start(bf16[64,2048]{1,0:T(8,128)(2,1)} %get-tuple-element.32), channel_id=1, source_target_pairs={{0,8},{8,0},{16,24},{24,16},{1,9},{9,1},{17,25},{25,17},{2,10},{10... | collective-permute-start | bytes 786440 | tf_op jit(solution)/shard_map/ppermute | solution.py:28
  80.0 12.5 %collective-permute-start.4 = (bf16[32,4096]{1,0:T(8,128)(2,1)S(1)}, bf16[32,4096]{1,0:T(8,128)(2,1)S(1)}, u32[]{:S(2)}, u32[]{:S(2)}) collective-permute-start(bf16[32,4096]{1,0:T(8,128)(2,1)S(1)} %copy-done.20), channel_id=1, source_target_pairs={{0,1},{1,0},{2,3},{3,2},{4,5},{5,4},{6,7},{7,6},{8,9},{9,8},{10,11... | collective-permute-start | bytes 786440 | tf_op jit(solution)/shard_map/ppermute | solution.py:28
  81.5 14.8 %collective-permute-start.6 = (bf16[32,4096]{1,0:T(8,128)(2,1)S(1)}, bf16[32,4096]{1,0:T(8,128)(2,1)}, u32[]{:S(2)}, u32[]{:S(2)}) collective-permute-start(bf16[32,4096]{1,0:T(8,128)(2,1)S(1)} %copy-done.19), channel_id=1, source_target_pairs={{0,1},{1,0},{2,3},{3,2},{4,5},{5,4},{6,7},{7,6},{8,9},{9,8},{10,11... | collective-permute-start | bytes 786440 | tf_op jit(solution)/shard_map/ppermute | solution.py:28
  82.0 28.8 %collective-permute-start.8 = (bf16[32,4096]{1,0:T(8,128)(2,1)}, bf16[32,4096]{1,0:T(8,128)(2,1)S(1)}, u32[]{:S(2)}, u32[]{:S(2)}) collective-permute-start(bf16[32,4096]{1,0:T(8,128)(2,1)} %get-tuple-element.29), channel_id=1, source_target_pairs={{0,1},{1,0},{2,3},{3,2},{4,5},{5,4},{6,7},{7,6},{8,9},{9,8},{10,11... | collective-permute-start | bytes 786440 | tf_op jit(solution)/shard_map/ppermute | solution.py:28
  84.3 29.4 %copy-start.15 = (bf16[32,4096]{1,0:T(8,128)(2,1)S(1)}, bf16[32,4096]{1,0:T(8,128)(2,1)}, u32[]{:S(2)}) copy-start(bf16[32,4096]{1,0:T(8,128)(2,1)} %get-tuple-element.28) | copy-start | bytes 786436
  84.3 18.9 %all-to-all-start = ((f32[16,32,128]{2,1,0:T(8,128)}), f32[16,32,128]{2,1,0:T(8,128)S(1)}, u32[]{:S(2)}, u32[]{:S(2)}) async-start(f32[16,32,128]{2,1,0:T(8,128)} %bitcast.6), calls=%async_computation | async-start | bytes 524288 | tf_op jit(solution)/shard_map/all_to_all | solution.py:60
  89.4 42.5 %collective-permute-start.3 = (bf16[32,4096]{1,0:T(8,128)(2,1)}, bf16[32,4096]{1,0:T(8,128)(2,1)S(1)}, u32[]{:S(2)}, u32[]{:S(2)}) collective-permute-start(bf16[32,4096]{1,0:T(8,128)(2,1)} %get-tuple-element.23), channel_id=1, source_target_pairs={{0,1},{1,0},{2,3},{3,2},{4,5},{5,4},{6,7},{7,6},{8,9},{9,8},{10,11... | collective-permute-start | bytes 786440 | tf_op jit(solution)/shard_map/ppermute | solution.py:28
  91.4 24.5 %copy-start.16 = (bf16[64,2048]{1,0:T(8,128)(2,1)S(1)}, bf16[64,2048]{1,0:T(8,128)(2,1)}, u32[]{:S(2)}) copy-start(bf16[64,2048]{1,0:T(8,128)(2,1)} %get-tuple-element.31) | copy-start | bytes 786436
  92.5 23.5 %collective-permute-start.19 = (bf16[64,2048]{1,0:T(8,128)(2,1)S(1)}, bf16[64,2048]{1,0:T(8,128)(2,1)}, u32[]{:S(2)}, u32[]{:S(2)}) collective-permute-start(bf16[64,2048]{1,0:T(8,128)(2,1)S(1)} %add_convert_fusion), channel_id=1, source_target_pairs={{0,16},{8,24},{16,0},{24,8},{1,17},{9,25},{17,1},{25,9},{2,18},{10... | collective-permute-start | bytes 786440 | tf_op jit(solution)/shard_map/ppermute | solution.py:28
  96.3 35.6 %collective-permute-start.5 = (bf16[32,4096]{1,0:T(8,128)(2,1)S(1)}, bf16[32,4096]{1,0:T(8,128)(2,1)S(1)}, u32[]{:S(2)}, u32[]{:S(2)}) collective-permute-start(bf16[32,4096]{1,0:T(8,128)(2,1)S(1)} %add_convert_fusion.3), channel_id=1, source_target_pairs={{0,2},{1,3},{2,0},{3,1},{4,6},{5,7},{6,4},{7,5},{8,10},{9,11},{10,... | collective-permute-start | bytes 786440 | tf_op jit(solution)/shard_map/ppermute | solution.py:28
  104.0 27.9 %all-to-all-start.1 = ((f32[16,32,128]{2,1,0:T(8,128)}), f32[16,32,128]{2,1,0:T(8,128)S(1)}, u32[]{:S(2)}, u32[]{:S(2)}) async-start(f32[16,32,128]{2,1,0:T(8,128)} %broadcast_in_dim.3), calls=%async_computation.1 | async-start | bytes 524288 | tf_op jit(solution)/shard_map/all_to_all | solution.py:62
  110.8 26.0 %collective-permute-start.7 = (bf16[32,4096]{1,0:T(8,128)(2,1)S(1)}, bf16[32,4096]{1,0:T(8,128)(2,1)}, u32[]{:S(2)}, u32[]{:S(2)}) collective-permute-start(bf16[32,4096]{1,0:T(8,128)(2,1)S(1)} %add_convert_fusion.2), channel_id=1, source_target_pairs={{0,4},{1,5},{2,6},{3,7},{4,0},{5,1},{6,2},{7,3},{8,12},{9,13},{10,... | collective-permute-start | bytes 786440 | tf_op jit(solution)/shard_map/ppermute | solution.py:28
  114.5 22.4 %collective-permute-start.9 = (bf16[32,4096]{1,0:T(8,128)(2,1)}, bf16[32,4096]{1,0:T(8,128)(2,1)}, u32[]{:S(2)}, u32[]{:S(2)}) collective-permute-start(bf16[32,4096]{1,0:T(8,128)(2,1)} %add_convert_fusion.1), channel_id=1, source_target_pairs={{0,6},{1,7},{2,4},{3,5},{4,2},{5,3},{6,0},{7,1},{8,14},{9,15},{10,... | collective-permute-start | bytes 786440 | tf_op jit(solution)/shard_map/ppermute | solution.py:28
  117.0 19.9 %copy-start.2 = (bf16[32,4096]{1,0:T(8,128)(2,1)S(1)}, bf16[32,4096]{1,0:T(8,128)(2,1)}, u32[]{:S(2)}) copy-start(bf16[32,4096]{1,0:T(8,128)(2,1)} %get-tuple-element.22.refs_13_) | copy-start | bytes 786436
  131.9 7.1 %collective-permute-start.21 = (f32[512,128]{1,0:T(8,128)S(1)}, f32[512,128]{1,0:T(8,128)S(1)}, u32[]{:S(2)}, u32[]{:S(2)}) collective-permute-start(f32[512,128]{1,0:T(8,128)S(1)} %bitcast.25), channel_id=1, source_target_pairs={{0,8},{8,0},{1,9},{9,1},{2,10},{10,2},{3,11},{11,3},{4,12},{12,4},... | collective-permute-start | bytes 786440 | tf_op jit(solution)/shard_map/ppermute | solution.py:28

commit v4 on v3

--- a/solution.py
+++ b/solution.py
@@ -57,12 +57,13 @@
     kept = kept + permute(sent, "core", 1)
     chips = ("far", "col")
     count = lax.axis_size("far") * lax.axis_size("col")
-    parts = lax.all_to_all(kept.reshape(count, half // count, -1), chips, 0, 0, tiled=True)
-    part = jnp.sum(parts, axis=0) * scale
+    parts = lax.all_to_all(kept.astype(BF16).reshape(count, half // count, -1), chips, 0, 0, tiled=True)
+    part = (jnp.sum(parts.astype(F32), axis=0) * scale).astype(BF16)
     parts = lax.all_to_all(jnp.broadcast_to(part, (count, *part.shape)), chips, 0, 0, tiled=True)
     kept = parts.reshape(half, -1)
     other = permute(kept, "core", 1)
-    return jnp.where(mine == 0, jnp.concatenate([kept, other]), jnp.concatenate([other, kept]))
+    whole = jnp.where(mine == 0, jnp.concatenate([kept, other]), jnp.concatenate([other, kept]))
+    return whole.astype(F32)
 
 
 def expand(pair_grad, out_weight, channels, blocks, earlier=()):

time: 142 us -> 132 us (0.930)
  waiting for transfers between devices: 35.6 us -> 28 us
    all_to_all x1, waiting for transfers between devices: 5.21 us -> 0.01 us  [reduce_everywhere(): lax.all_to_all(kept.astype(BF16).reshape(count, half // count, -1), chips...]
    all_to_all x1, waiting for transfers between devices: 12.5 us -> 10.3 us  [reduce_everywhere(): lax.all_to_all(jnp.broadcast_to(part, (count, *part.shape)), chips, 0, 0,...]
    all_to_all x1, starting transfers between devices: 6.81 us -> 4.78 us  [reduce_everywhere(): lax.all_to_all(jnp.broadcast_to(part, (count, *part.shape)), chips, 0, 0,...]
    convert_element_type x0 -> x3, other arithmetic: none -> 1.54 us  [the longest x1 0.86 us: reduce_everywhere(): return whole.astype(F32)]
    unnamed x46 -> x44, local copies, waits for them, and re-layouts: 8.5 us -> 8.49 us
  transfers between devices with their start and end apart: 24 -> 24, of which waited for: 7 -> 6; matrix products, arithmetic and copies ran while one was open for 8% -> 8% of each run, Pallas kernels for 26% -> 28%
where the time goes in v4:
time: 132 us; the launch traced here: 130 us
  Pallas kernels  50.2 us (38%)
  starting transfers between devices  35.4 us (27%)
  waiting for transfers between devices  28 us (21%)
  local copies, waits for them, and re-layouts  9.8 us (7%)
  other arithmetic  5.73 us (4%)
    ppermute x22, starting transfers between devices, permute(): return lax.ppermute(array, axis, toggled(axis, bit))  25.5 us
    ppermute x22, waiting for transfers between devices, permute(): return lax.ppermute(array, axis, toggled(axis, bit))  17.7 us
    pallas_call x2, Pallas kernels, expand(): pl.pallas_call(kernel, grid=(count,), in_specs=[pl.BlockSpec((rows, BLOCK...  15.7 us
    pallas_call x2, Pallas kernels, weight_product(): pl.pallas_call(kernel, grid=(count,), in_specs=[pl.BlockSpec(memory_space...  14.3 us
    all_to_all x1, waiting for transfers between devices, reduce_everywhere(): lax.all_to_all(jnp.broadcast_to(part, (count, *part.shape)), chips, 0, 0,...  10.3 us
    pallas_call x1, Pallas kernels, right_product(): pl.pallas_call(kernel, grid=(depth // tile,), in_specs=[pl.BlockSpec(memo...  10.1 us
    pallas_call x1, Pallas kernels, left_product(): pl.pallas_call(kernel, grid=(width // tile,), in_specs=[pl.BlockSpec(memo...  10.1 us
    unnamed x44, local copies, waits for them, and re-layouts  8.49 us
  transfers between devices with their start and end apart: 24, of which 6 were waited for; matrix products, arithmetic and copies ran while one was open for 8% of the time, Pallas kernels for 28%

profile of v4, /device:TPU:0, one launch (start us, length us, event | category | flops | bytes accessed | tf_op | source)
XLA Modules:
  0.0 130.1 jit_solution(3607837277687362158)
XLA Ops:
  0.6 2.1 %copy.11 = bf16[64,64,32]{0,2,1:T(8,128)(2,1)S(1)} copy(bf16[64,64,32]{1,2,0:T(8,128)(2,1)} %param.5) | data formatting | bytes 524288 | tf_op args[1]
  2.8 0.2 copy.14.refs_0_.refs_8_
  3.0 0.0 copy-start.3
  3.0 3.1 %collective-permute-start.1 = (bf16[64,2048]{1,0:T(8,128)(2,1)S(1)}, bf16[64,2048]{1,0:T(8,128)(2,1)S(1)}, u32[]{:S(2)}, u32[]{:S(2)}) collective-permute-start(bf16[64,2048]{1,0:T(8,128)(2,1)S(1)} %copy.14.refs_0_.refs_8_), channel_id=1, source_target_pairs={{0,16},{8,24},{16,0},{24,8},{1,17},{9,25},{17,1},{25,9},{2,18},{10... | collective-permute-start | bytes 786440 | tf_op jit(solution)/shard_map/ppermute | solution.py:28
  6.0 1.1 copy.22
  7.1 1.6 %collective-permute-start.11 = (bf16[32,4096]{1,0:T(8,128)(2,1)S(1)}, bf16[32,4096]{1,0:T(8,128)(2,1)S(1)}, u32[]{:S(2)}, u32[]{:S(2)}) collective-permute-start(bf16[32,4096]{1,0:T(8,128)(2,1)S(1)} %bitcast.18), channel_id=1, source_target_pairs={{0,2},{1,3},{2,0},{3,1},{4,6},{5,7},{6,4},{7,5},{8,10},{9,11},{10,... | collective-permute-start | bytes 786440 | tf_op jit(solution)/shard_map/ppermute | solution.py:28
  8.8 2.6 %collective-permute-start.13 = (bf16[32,4096]{1,0:T(8,128)(2,1)S(1)}, bf16[32,4096]{1,0:T(8,128)(2,1)S(1)}, u32[]{:S(2)}, u32[]{:S(2)}) collective-permute-start(bf16[32,4096]{1,0:T(8,128)(2,1)S(1)} %bitcast.19), channel_id=1, source_target_pairs={{0,4},{1,5},{2,6},{3,7},{4,0},{5,1},{6,2},{7,3},{8,12},{9,13},{10,... | collective-permute-start | bytes 786440 | tf_op jit(solution)/shard_map/ppermute | solution.py:28
  11.3 0.2 collective-permute-start.15
  11.6 7.9 %expand.2 = (bf16[2048,4096]{1,0:T(8,128)(2,1)}, bf16[64,128,128]{2,1,0:T(8,128)(2,1)}) custom-call(bf16[128,64,128]{2,1,0:T(8,128)(2,1)} %refs_0_.3, bf16[1024,128]{1,0:T(8,128)(2,1)} %refs_1_.3), custom_call_target="tpu_custom_call" | custom-call | flops 2147483648 | bytes 8388608 | tf_op jit(solution)/shard_map/expand/pallas_call | solution.py:98
  19.5 0.0 collective-permute-done.1.refs_2_.refs_10_
  19.5 0.0 copy-start.8
  19.5 0.1 collective-permute-start.2
  19.6 0.1 pad_add_fusion.own_ref
  19.7 0.1 rev.3.own_ref
  19.8 7.8 %expand.3 = (bf16[2048,4096]{1,0:T(8,128)(2,1)}, bf16[64,128,128]{2,1,0:T(8,128)(2,1)}) custom-call(bf16[128,64,128]{2,1,0:T(8,128)(2,1)} %refs_0_.3, bf16[1024,128]{1,0:T(8,128)(2,1)} %refs_1_.3, bf16[2048,4096]{1,0:T(8,128)(2,1)} %get-tuple-element.19.refs_2_, ...), custom_call_target="tpu_custom_call", output_to_operand_aliasing={{0}: (2, {}), {1}: (3, {})} | custom-call | flops 2147483648 | bytes 8388608 | tf_op jit(solution)/shard_map/expand/pallas_call | solution.py:98
  27.6 0.0 copy-start.9
  27.6 1.6 %collective-permute-start.10 = (bf16[32,4096]{1,0:T(8,128)(2,1)S(1)}, bf16[32,4096]{1,0:T(8,128)(2,1)S(1)}, u32[]{:S(2)}, u32[]{:S(2)}) collective-permute-start(bf16[32,4096]{1,0:T(8,128)(2,1)S(1)} %bitcast.21), channel_id=1, source_target_pairs={{0,1},{1,0},{2,3},{3,2},{4,5},{5,4},{6,7},{7,6},{8,9},{9,8},{10,11... | collective-permute-start | bytes 786440 | tf_op jit(solution)/shard_map/ppermute | solution.py:28
  29.2 0.0 collective-permute-done.11.refs_2_
  29.2 0.5 collective-permute-start.12
  29.7 0.4 collective-permute-done.13.refs_4_
  30.1 1.5 %collective-permute-start.14 = (bf16[32,4096]{1,0:T(8,128)(2,1)S(1)}, bf16[32,4096]{1,0:T(8,128)(2,1)S(1)}, u32[]{:S(2)}, u32[]{:S(2)}) collective-permute-start(bf16[32,4096]{1,0:T(8,128)(2,1)S(1)} %collective-permute-done.13.refs_4_), channel_id=1, source_target_pairs={{0,1},{1,0},{2,3},{3,2},{4,5},{5,4},{6,7},{7,6},{8,9},{9,8},{10,11... | collective-permute-start | bytes 786440 | tf_op jit(solution)/shard_map/ppermute | solution.py:28
  31.6 0.0 collective-permute-done.15.refs_6_
  31.6 0.5 collective-permute-start.16
  32.2 0.7 copy-done.10
  32.9 10.1 %left.1 = (bf16[32,4096]{1,0:T(8,128)(2,1)}, bf16[32,4096]{1,0:T(8,128)(2,1)}, bf16[32,4096]{1,0:T(8,128)(2,1)}, bf16[32,4096]{1,0:T(8,128)(2,1)}, bf16[32,4096]...) custom-call(s32[2]{0:T(128)S(1)} %pad_add_fusion.own_ref, ...), custom_call_target="tpu_custom_call" | custom-call | flops 4294967296 | bytes 16777216 | tf_op jit(solution)/shard_map/left/pallas_call | solution.py:160
  43.0 0.0 collective-permute-done.10.refs_1_
  43.0 5.1 %collective-permute-done.14.refs_5_ = bf16[32,4096]{1,0:T(8,128)(2,1)S(1)} collective-permute-done((bf16[32,4096]{1,0:T(8,128)(2,1)S(1)}, bf16[32,4096]{1,0:T(8,128)(2,1)S(1)}, u32[]{:S(2)}, u32[]{:S(2)}) %collective-permute-start.14) | collective-permute-done | bytes 262176 | tf_op jit(solution)/shard_map/ppermute | solution.py:28
  48.1 5.1 %collective-permute-done.16.refs_7_ = bf16[32,4096]{1,0:T(8,128)(2,1)S(1)} collective-permute-done((bf16[32,4096]{1,0:T(8,128)(2,1)S(1)}, bf16[32,4096]{1,0:T(8,128)(2,1)S(1)}, u32[]{:S(2)}, u32[]{:S(2)}) %collective-permute-start.16) | collective-permute-done | bytes 262176 | tf_op jit(solution)/shard_map/ppermute | solution.py:28
  53.2 0.7 copy-done.14
  54.0 0.9 copy-done.1
  54.9 7.1 %weight.2.refs_13_.refs_14_ = f32[1024,128]{1,0:T(8,128)S(1)} custom-call(s32[2]{0:T(128)S(1)} %pad_add_fusion.own_ref, bf16[32,4096]{1,0:T(8,128)(2,1)} %bitcast.22, bf16[32,4096]{1,0:T(8,128)(2,1)} %copy-done.11, bf16[32,4096]{1,0:T(8,128)(2,1)} %copy-done.5, bf16[32,4096]{1,0:T(8,128)(2,1)} %copy-done.12, bf16[32,4096]{1,0:T(8,128)(2,1)} %copy-done.6, ...), custom_call_target="tpu_custom_call" | custom-call | flops 6442450944 | bytes 2097152 | tf_op jit(solution)/shard_map/weight/pallas_call | solution.py:250
  62.0 7.2 %weight.3.refs_9_ = f32[1024,128]{1,0:T(8,128)S(1)} custom-call(s32[2]{0:T(128)S(1)} %pad_add_fusion.own_ref, bf16[32,4096]{1,0:T(8,128)(2,1)} %bitcast.23, bf16[32,4096]{1,0:T(8,128)(2,1)} %copy-done.11, bf16[32,4096]{1,0:T(8,128)(2,1)} %copy-done.5, bf16[32,4096]{1,0:T(8,128)(2,1)} %copy-done.12, bf16[32,4096]{1,0:T(8,128)(2,1)} %copy-done.6, ...), custom_call_target="tpu_custom_call" | custom-call | flops 6442450944 | bytes 2097152 | tf_op jit(solution)/shard_map/weight/pallas_call | solution.py:250
  69.3 0.1 collective-permute-start.20
  69.3 10.1 %right.1 = (bf16[64,2048]{1,0:T(8,128)(2,1)}, bf16[64,2048]{1,0:T(8,128)(2,1)}, bf16[64,2048]{1,0:T(8,128)(2,1)}, bf16[64,2048]{1,0:T(8,128)(2,1)}) custom-call(s32[2]{0:T(128)S(1)} %rev.3.own_ref, bf16[32,4096]{1,0:T(8,128)(2,1)} %bitcast.24, bf16[32,4096]{1,0:T(8,128)(2,1)} %copy-done.11, bf16[32,4096]{1,0:T(8,128)(2,1)} %copy-done.5, ...), custom_call_target="tpu_custom_call" | custom-call | flops 4294967296 | bytes 16777216 | tf_op jit(solution)/shard_map/right/pallas_call | solution.py:195
  79.5 0.5 collective-permute-start.18
  80.0 0.1 collective-permute-start.17
  80.0 1.5 %collective-permute-start.4 = (bf16[32,4096]{1,0:T(8,128)(2,1)}, bf16[32,4096]{1,0:T(8,128)(2,1)S(1)}, u32[]{:S(2)}, u32[]{:S(2)}) collective-permute-start(bf16[32,4096]{1,0:T(8,128)(2,1)} %get-tuple-element.25), channel_id=1, source_target_pairs={{0,1},{1,0},{2,3},{3,2},{4,5},{5,4},{6,7},{7,6},{8,9},{9,8},{10,11... | collective-permute-start | bytes 786440 | tf_op jit(solution)/shard_map/ppermute | solution.py:28
  81.5 0.5 collective-permute-start.6
  82.1 1.5 %collective-permute-start.8 = (bf16[32,4096]{1,0:T(8,128)(2,1)}, bf16[32,4096]{1,0:T(8,128)(2,1)}, u32[]{:S(2)}, u32[]{:S(2)}) collective-permute-start(bf16[32,4096]{1,0:T(8,128)(2,1)} %get-tuple-element.29), channel_id=1, source_target_pairs={{0,1},{1,0},{2,3},{3,2},{4,5},{5,4},{6,7},{7,6},{8,9},{9,8},{10,11... | collective-permute-start | bytes 786440 | tf_op jit(solution)/shard_map/ppermute | solution.py:28
  83.6 0.7 add_convert_fusion.4
  84.2 5.1 %all-to-all-start = ((bf16[16,32,128]{2,1,0:T(8,128)(2,1)}), bf16[16,32,128]{2,1,0:T(8,128)(2,1)S(1)}, u32[]{:S(2)}, u32[]{:S(2)}) async-start(bf16[16,32,128]{2,1,0:T(8,128)(2,1)} %bitcast.6), calls=%async_computation | async-start | bytes 262144 | tf_op jit(solution)/shard_map/all_to_all | solution.py:60
  89.4 0.0 collective-permute-done.18
  89.4 2.0 %collective-permute-start.3 = (bf16[32,4096]{1,0:T(8,128)(2,1)}, bf16[32,4096]{1,0:T(8,128)(2,1)S(1)}, u32[]{:S(2)}, u32[]{:S(2)}) collective-permute-start(bf16[32,4096]{1,0:T(8,128)(2,1)} %get-tuple-element.23), channel_id=1, source_target_pairs={{0,1},{1,0},{2,3},{3,2},{4,5},{5,4},{6,7},{7,6},{8,9},{9,8},{10,11... | collective-permute-start | bytes 786440 | tf_op jit(solution)/shard_map/ppermute | solution.py:28
  91.4 1.0 add_convert_fusion
  92.4 1.5 %collective-permute-start.19 = (bf16[64,2048]{1,0:T(8,128)(2,1)S(1)}, bf16[64,2048]{1,0:T(8,128)(2,1)}, u32[]{:S(2)}, u32[]{:S(2)}) collective-permute-start(bf16[64,2048]{1,0:T(8,128)(2,1)S(1)} %add_convert_fusion), channel_id=1, source_target_pairs={{0,16},{8,24},{16,0},{24,8},{1,17},{9,25},{17,1},{25,9},{2,18},{10... | collective-permute-start | bytes 786440 | tf_op jit(solution)/shard_map/ppermute | solution.py:28
  93.9 0.1 add_convert_fusion.3
  94.0 1.9 %collective-permute-done.6 = bf16[32,4096]{1,0:T(8,128)(2,1)S(1)} collective-permute-done((bf16[32,4096]{1,0:T(8,128)(2,1)S(1)}, bf16[32,4096]{1,0:T(8,128)(2,1)S(1)}, u32[]{:S(2)}, u32[]{:S(2)}) %collective-permute-start.6) | collective-permute-done | bytes 262176 | tf_op jit(solution)/shard_map/ppermute | solution.py:28
  95.9 0.7 collective-permute-start.5
  96.6 0.1 add_convert_fusion.2
  96.7 5.2 %collective-permute-done.8 = bf16[32,4096]{1,0:T(8,128)(2,1)} collective-permute-done((bf16[32,4096]{1,0:T(8,128)(2,1)}, bf16[32,4096]{1,0:T(8,128)(2,1)}, u32[]{:S(2)}, u32[]{:S(2)}) %collective-permute-start.8) | collective-permute-done | bytes 262176 | tf_op jit(solution)/shard_map/ppermute | solution.py:28
  101.8 1.7 %collective-permute-start.7 = (bf16[32,4096]{1,0:T(8,128)(2,1)S(1)}, bf16[32,4096]{1,0:T(8,128)(2,1)S(1)}, u32[]{:S(2)}, u32[]{:S(2)}) collective-permute-start(bf16[32,4096]{1,0:T(8,128)(2,1)S(1)} %add_convert_fusion.2), channel_id=1, source_target_pairs={{0,4},{1,5},{2,6},{3,7},{4,0},{5,1},{6,2},{7,3},{8,12},{9,13},{10,... | collective-permute-start | bytes 786440 | tf_op jit(solution)/shard_map/ppermute | solution.py:28
  103.5 1.7 %add_convert_fusion.1 = bf16[32,4096]{1,0:T(8,128)(2,1)} fusion(bf16[32,4096]{1,0:T(8,128)(2,1)} %collective-permute-done.8, bf16[32,4096]{1,0:T(8,128)(2,1)S(1)} %copy-done.15), kind=kLoop, calls=%fused_computation.3 | loop fusion | flops 524288 | bytes 786432 | tf_op jit(solution)/shard_map/convert_element_type | solution.py:48
  105.3 0.7 broadcast_in_dim.3
  105.9 4.8 %all-to-all-start.1 = ((bf16[16,32,128]{2,1,0:T(8,128)(2,1)}), bf16[16,32,128]{2,1,0:T(8,128)(2,1)S(1)}, u32[]{:S(2)}, u32[]{:S(2)}) async-start(bf16[16,32,128]{2,1,0:T(8,128)(2,1)} %broadcast_in_dim.3), calls=%async_computation.1 | async-start | bytes 262144 | tf_op jit(solution)/shard_map/all_to_all | solution.py:62
  110.7 3.8 %collective-permute-start.9 = (bf16[32,4096]{1,0:T(8,128)(2,1)}, bf16[32,4096]{1,0:T(8,128)(2,1)S(1)}, u32[]{:S(2)}, u32[]{:S(2)}) collective-permute-start(bf16[32,4096]{1,0:T(8,128)(2,1)} %add_convert_fusion.1), channel_id=1, source_target_pairs={{0,6},{1,7},{2,4},{3,5},{4,2},{5,3},{6,0},{7,1},{8,14},{9,15},{10,... | collective-permute-start | bytes 786440 | tf_op jit(solution)/shard_map/ppermute | solution.py:28
  114.5 0.0 collective-permute-done.19
  114.5 1.1 add_multiply_fusion
  115.6 10.3 %all-to-all-done.1 = bf16[16,32,128]{2,1,0:T(8,128)(2,1)S(1)} async-done(((bf16[16,32,128]{2,1,0:T(8,128)(2,1)}), bf16[16,32,128]{2,1,0:T(8,128)(2,1)S(1)}, u32[]{:S(2)}, u32[]{:S(2)}) %all-to-all-start.1) | async-done | bytes 131104 | tf_op jit(solution)/shard_map/all_to_all | solution.py:62
  125.8 0.0 collective-permute-done.3
  125.9 0.2 multiply_bitcast_fusion
  126.1 0.3 copy.17
  126.4 2.0 %copy.18 = f32[64,64,32]{1,2,0:T(8,128)} copy(f32[64,64,32]{0,2,1:T(8,128)S(1)} %bitcast.16) | data formatting | bytes 1048576
  128.4 0.9 copy.19
  129.3 0.9 fusion
  (50 shorter events, 0.2 us)
Async XLA Ops:
  3.0 16.5 %copy-start.3 = (bf16[64,2048]{1,0:T(8,128)(2,1)}, bf16[64,2048]{1,0:T(8,128)(2,1)S(1)}, u32[]{:S(2)}) copy-start(bf16[64,2048]{1,0:T(8,128)(2,1)S(1)} %copy.14.refs_0_.refs_8_) | copy-start | bytes 786436
  3.0 16.5 %collective-permute-start.1 = (bf16[64,2048]{1,0:T(8,128)(2,1)S(1)}, bf16[64,2048]{1,0:T(8,128)(2,1)S(1)}, u32[]{:S(2)}, u32[]{:S(2)}) collective-permute-start(bf16[64,2048]{1,0:T(8,128)(2,1)S(1)} %copy.14.refs_0_.refs_8_), channel_id=1, source_target_pairs={{0,16},{8,24},{16,0},{24,8},{1,17},{9,25},{17,1},{25,9},{2,18},{10... | collective-permute-start | bytes 786440 | tf_op jit(solution)/shard_map/ppermute | solution.py:28
  6.0 21.5 %collective-permute-start = (bf16[64,2048]{1,0:T(8,128)(2,1)S(1)}, bf16[64,2048]{1,0:T(8,128)(2,1)S(1)}, u32[]{:S(2)}, u32[]{:S(2)}) collective-permute-start(bf16[64,2048]{1,0:T(8,128)(2,1)S(1)} %copy.14.refs_0_.refs_8_), channel_id=1, source_target_pairs={{0,8},{8,0},{16,24},{24,16},{1,9},{9,1},{17,25},{25,17},{2,10},{10... | collective-permute-start | bytes 786440 | tf_op jit(solution)/shard_map/ppermute | solution.py:28
  7.1 20.5 %copy-start.4 = (bf16[4,8,32,128]{3,1,2,0:T(8,128)(2,1)}, bf16[4,8,32,128]{3,1,2,0:T(8,128)(2,1)S(1)}, u32[]{:S(2)}) copy-start(bf16[4,8,32,128]{3,1,2,0:T(8,128)(2,1)S(1)} %copy.22) | copy-start | bytes 786436
  7.1 22.1 %collective-permute-start.11 = (bf16[32,4096]{1,0:T(8,128)(2,1)S(1)}, bf16[32,4096]{1,0:T(8,128)(2,1)S(1)}, u32[]{:S(2)}, u32[]{:S(2)}) collective-permute-start(bf16[32,4096]{1,0:T(8,128)(2,1)S(1)} %bitcast.18), channel_id=1, source_target_pairs={{0,2},{1,3},{2,0},{3,1},{4,6},{5,7},{6,4},{7,5},{8,10},{9,11},{10,... | collective-permute-start | bytes 786440 | tf_op jit(solution)/shard_map/ppermute | solution.py:28
  8.8 21.4 %collective-permute-start.13 = (bf16[32,4096]{1,0:T(8,128)(2,1)S(1)}, bf16[32,4096]{1,0:T(8,128)(2,1)S(1)}, u32[]{:S(2)}, u32[]{:S(2)}) collective-permute-start(bf16[32,4096]{1,0:T(8,128)(2,1)S(1)} %bitcast.19), channel_id=1, source_target_pairs={{0,4},{1,5},{2,6},{3,7},{4,0},{5,1},{6,2},{7,3},{8,12},{9,13},{10,... | collective-permute-start | bytes 786440 | tf_op jit(solution)/shard_map/ppermute | solution.py:28
  11.3 20.3 %collective-permute-start.15 = (bf16[32,4096]{1,0:T(8,128)(2,1)S(1)}, bf16[32,4096]{1,0:T(8,128)(2,1)S(1)}, u32[]{:S(2)}, u32[]{:S(2)}) collective-permute-start(bf16[32,4096]{1,0:T(8,128)(2,1)S(1)} %bitcast.20), channel_id=1, source_target_pairs={{0,6},{1,7},{2,4},{3,5},{4,2},{5,3},{6,0},{7,1},{8,14},{9,15},{10,... | collective-permute-start | bytes 786440 | tf_op jit(solution)/shard_map/ppermute | solution.py:28
  19.5 8.1 %copy-start.8 = (bf16[64,2048]{1,0:T(8,128)(2,1)}, bf16[64,2048]{1,0:T(8,128)(2,1)S(1)}, u32[]{:S(2)}) copy-start(bf16[64,2048]{1,0:T(8,128)(2,1)S(1)} %collective-permute-done.1.refs_2_.refs_10_) | copy-start | bytes 786436
  19.5 12.7 %collective-permute-start.2 = (bf16[64,2048]{1,0:T(8,128)(2,1)S(1)}, bf16[64,2048]{1,0:T(8,128)(2,1)S(1)}, u32[]{:S(2)}, u32[]{:S(2)}) collective-permute-start(bf16[64,2048]{1,0:T(8,128)(2,1)S(1)} %collective-permute-done.1.refs_2_.refs_10_), channel_id=1, source_target_pairs={{0,8},{8,0},{16,24},{24,16},{1,9},{9,1},{17,25},{25,17},{2,10},{10... | collective-permute-start | bytes 786440 | tf_op jit(solution)/shard_map/ppermute | solution.py:28
  27.6 4.6 %copy-start.9 = (bf16[64,2048]{1,0:T(8,128)(2,1)}, bf16[64,2048]{1,0:T(8,128)(2,1)S(1)}, u32[]{:S(2)}) copy-start(bf16[64,2048]{1,0:T(8,128)(2,1)S(1)} %collective-permute-done.refs_1_.refs_9_) | copy-start | bytes 786436
  27.6 15.4 %collective-permute-start.10 = (bf16[32,4096]{1,0:T(8,128)(2,1)S(1)}, bf16[32,4096]{1,0:T(8,128)(2,1)S(1)}, u32[]{:S(2)}, u32[]{:S(2)}) collective-permute-start(bf16[32,4096]{1,0:T(8,128)(2,1)S(1)} %bitcast.21), channel_id=1, source_target_pairs={{0,1},{1,0},{2,3},{3,2},{4,5},{5,4},{6,7},{7,6},{8,9},{9,8},{10,11... | collective-permute-start | bytes 786440 | tf_op jit(solution)/shard_map/ppermute | solution.py:28
  29.2 13.8 %copy-start.5 = (bf16[32,4096]{1,0:T(8,128)(2,1)}, bf16[32,4096]{1,0:T(8,128)(2,1)S(1)}, u32[]{:S(2)}) copy-start(bf16[32,4096]{1,0:T(8,128)(2,1)S(1)} %collective-permute-done.11.refs_2_) | copy-start | bytes 786436
  29.2 13.8 %collective-permute-start.12 = (bf16[32,4096]{1,0:T(8,128)(2,1)S(1)}, bf16[32,4096]{1,0:T(8,128)(2,1)S(1)}, u32[]{:S(2)}, u32[]{:S(2)}) collective-permute-start(bf16[32,4096]{1,0:T(8,128)(2,1)S(1)} %collective-permute-done.11.refs_2_), channel_id=1, source_target_pairs={{0,1},{1,0},{2,3},{3,2},{4,5},{5,4},{6,7},{7,6},{8,9},{9,8},{10,11... | collective-permute-start | bytes 786440 | tf_op jit(solution)/shard_map/ppermute | solution.py:28
  30.1 12.9 %copy-start.6 = (bf16[32,4096]{1,0:T(8,128)(2,1)}, bf16[32,4096]{1,0:T(8,128)(2,1)S(1)}, u32[]{:S(2)}) copy-start(bf16[32,4096]{1,0:T(8,128)(2,1)S(1)} %collective-permute-done.13.refs_4_) | copy-start | bytes 786436
  30.1 18.0 %collective-permute-start.14 = (bf16[32,4096]{1,0:T(8,128)(2,1)S(1)}, bf16[32,4096]{1,0:T(8,128)(2,1)S(1)}, u32[]{:S(2)}, u32[]{:S(2)}) collective-permute-start(bf16[32,4096]{1,0:T(8,128)(2,1)S(1)} %collective-permute-done.13.refs_4_), channel_id=1, source_target_pairs={{0,1},{1,0},{2,3},{3,2},{4,5},{5,4},{6,7},{7,6},{8,9},{9,8},{10,11... | collective-permute-start | bytes 786440 | tf_op jit(solution)/shard_map/ppermute | solution.py:28
  31.6 11.4 %copy-start.7 = (bf16[32,4096]{1,0:T(8,128)(2,1)}, bf16[32,4096]{1,0:T(8,128)(2,1)S(1)}, u32[]{:S(2)}) copy-start(bf16[32,4096]{1,0:T(8,128)(2,1)S(1)} %collective-permute-done.15.refs_6_) | copy-start | bytes 786436
  31.6 21.6 %collective-permute-start.16 = (bf16[32,4096]{1,0:T(8,128)(2,1)S(1)}, bf16[32,4096]{1,0:T(8,128)(2,1)S(1)}, u32[]{:S(2)}, u32[]{:S(2)}) collective-permute-start(bf16[32,4096]{1,0:T(8,128)(2,1)S(1)} %collective-permute-done.15.refs_6_), channel_id=1, source_target_pairs={{0,1},{1,0},{2,3},{3,2},{4,5},{5,4},{6,7},{7,6},{8,9},{9,8},{10,11... | collective-permute-start | bytes 786440 | tf_op jit(solution)/shard_map/ppermute | solution.py:28
  32.2 0.7 copy-start.10
  32.9 21.1 %copy-start = (bf16[64,128,128]{2,1,0:T(8,128)(2,1)S(1)}, bf16[64,128,128]{2,1,0:T(8,128)(2,1)}, u32[]{:S(2)}) copy-start(bf16[64,128,128]{2,1,0:T(8,128)(2,1)} %get-tuple-element.30.refs_12_) | copy-start | bytes 6291460
  43.0 10.2 %copy-start.11 = (bf16[32,4096]{1,0:T(8,128)(2,1)}, bf16[32,4096]{1,0:T(8,128)(2,1)S(1)}, u32[]{:S(2)}) copy-start(bf16[32,4096]{1,0:T(8,128)(2,1)S(1)} %collective-permute-done.10.refs_1_) | copy-start | bytes 786436
  43.0 10.2 %copy-start.12 = (bf16[32,4096]{1,0:T(8,128)(2,1)}, bf16[32,4096]{1,0:T(8,128)(2,1)S(1)}, u32[]{:S(2)}) copy-start(bf16[32,4096]{1,0:T(8,128)(2,1)S(1)} %collective-permute-done.12.refs_3_) | copy-start | bytes 786436
  48.1 5.2 %copy-start.13 = (bf16[32,4096]{1,0:T(8,128)(2,1)}, bf16[32,4096]{1,0:T(8,128)(2,1)S(1)}, u32[]{:S(2)}) copy-start(bf16[32,4096]{1,0:T(8,128)(2,1)S(1)} %collective-permute-done.14.refs_5_) | copy-start | bytes 786436
  53.2 0.7 copy-start.14
  54.0 1.0 copy-start.1
  69.2 12.3 %copy-start.19 = (bf16[32,4096]{1,0:T(8,128)(2,1)S(1)}, bf16[32,4096]{1,0:T(8,128)(2,1)}, u32[]{:S(2)}) copy-start(bf16[32,4096]{1,0:T(8,128)(2,1)} %get-tuple-element.27) | copy-start | bytes 786436
  69.3 24.7 %copy-start.18 = (bf16[32,4096]{1,0:T(8,128)(2,1)S(1)}, bf16[32,4096]{1,0:T(8,128)(2,1)}, u32[]{:S(2)}) copy-start(bf16[32,4096]{1,0:T(8,128)(2,1)} %get-tuple-element.24) | copy-start | bytes 786436
  69.3 12.8 %collective-permute-start.20 = (f32[512,128]{1,0:T(8,128)S(1)}, f32[512,128]{1,0:T(8,128)S(1)}, u32[]{:S(2)}, u32[]{:S(2)}) collective-permute-start(f32[512,128]{1,0:T(8,128)S(1)} %constant_dynamic-slice_fusion), channel_id=1, source_target_pairs={{0,8},{8,0},{1,9},{9,1},{2,10},{10,2},{3,11},{11,3},{4,12},{12,4},... | collective-permute-start | bytes 786440 | tf_op jit(solution)/shard_map/ppermute | solution.py:28
  79.4 17.2 %copy-start.17 = (bf16[32,4096]{1,0:T(8,128)(2,1)S(1)}, bf16[32,4096]{1,0:T(8,128)(2,1)}, u32[]{:S(2)}) copy-start(bf16[32,4096]{1,0:T(8,128)(2,1)} %get-tuple-element.26) | copy-start | bytes 786436
  79.5 24.1 %copy-start.15 = (bf16[32,4096]{1,0:T(8,128)(2,1)S(1)}, bf16[32,4096]{1,0:T(8,128)(2,1)}, u32[]{:S(2)}) copy-start(bf16[32,4096]{1,0:T(8,128)(2,1)} %get-tuple-element.28) | copy-start | bytes 786436
  79.5 9.9 %collective-permute-start.18 = (bf16[64,2048]{1,0:T(8,128)(2,1)}, bf16[64,2048]{1,0:T(8,128)(2,1)S(1)}, u32[]{:S(2)}, u32[]{:S(2)}) collective-permute-start(bf16[64,2048]{1,0:T(8,128)(2,1)} %get-tuple-element.34), channel_id=1, source_target_pairs={{0,8},{8,0},{16,24},{24,16},{1,9},{9,1},{17,25},{25,17},{2,10},{10... | collective-permute-start | bytes 786440 | tf_op jit(solution)/shard_map/ppermute | solution.py:28
  80.0 30.8 %collective-permute-start.17 = (bf16[64,2048]{1,0:T(8,128)(2,1)}, bf16[64,2048]{1,0:T(8,128)(2,1)S(1)}, u32[]{:S(2)}, u32[]{:S(2)}) collective-permute-start(bf16[64,2048]{1,0:T(8,128)(2,1)} %get-tuple-element.32), channel_id=1, source_target_pairs={{0,8},{8,0},{16,24},{24,16},{1,9},{9,1},{17,25},{25,17},{2,10},{10... | collective-permute-start | bytes 786440 | tf_op jit(solution)/shard_map/ppermute | solution.py:28
  80.0 12.3 %collective-permute-start.4 = (bf16[32,4096]{1,0:T(8,128)(2,1)}, bf16[32,4096]{1,0:T(8,128)(2,1)S(1)}, u32[]{:S(2)}, u32[]{:S(2)}) collective-permute-start(bf16[32,4096]{1,0:T(8,128)(2,1)} %get-tuple-element.25), channel_id=1, source_target_pairs={{0,1},{1,0},{2,3},{3,2},{4,5},{5,4},{6,7},{7,6},{8,9},{9,8},{10,11... | collective-permute-start | bytes 786440 | tf_op jit(solution)/shard_map/ppermute | solution.py:28
  81.5 14.4 %collective-permute-start.6 = (bf16[32,4096]{1,0:T(8,128)(2,1)S(1)}, bf16[32,4096]{1,0:T(8,128)(2,1)S(1)}, u32[]{:S(2)}, u32[]{:S(2)}) collective-permute-start(bf16[32,4096]{1,0:T(8,128)(2,1)S(1)} %copy-done.19), channel_id=1, source_target_pairs={{0,1},{1,0},{2,3},{3,2},{4,5},{5,4},{6,7},{7,6},{8,9},{9,8},{10,11... | collective-permute-start | bytes 786440 | tf_op jit(solution)/shard_map/ppermute | solution.py:28
  82.1 19.8 %collective-permute-start.8 = (bf16[32,4096]{1,0:T(8,128)(2,1)}, bf16[32,4096]{1,0:T(8,128)(2,1)}, u32[]{:S(2)}, u32[]{:S(2)}) collective-permute-start(bf16[32,4096]{1,0:T(8,128)(2,1)} %get-tuple-element.29), channel_id=1, source_target_pairs={{0,1},{1,0},{2,3},{3,2},{4,5},{5,4},{6,7},{7,6},{8,9},{9,8},{10,11... | collective-permute-start | bytes 786440 | tf_op jit(solution)/shard_map/ppermute | solution.py:28
  84.2 30.3 %copy-start.16 = (bf16[64,2048]{1,0:T(8,128)(2,1)S(1)}, bf16[64,2048]{1,0:T(8,128)(2,1)}, u32[]{:S(2)}) copy-start(bf16[64,2048]{1,0:T(8,128)(2,1)} %get-tuple-element.31) | copy-start | bytes 786436
  84.2 21.0 %all-to-all-start = ((bf16[16,32,128]{2,1,0:T(8,128)(2,1)}), bf16[16,32,128]{2,1,0:T(8,128)(2,1)S(1)}, u32[]{:S(2)}, u32[]{:S(2)}) async-start(bf16[16,32,128]{2,1,0:T(8,128)(2,1)} %bitcast.6), calls=%async_computation | async-start | bytes 262144 | tf_op jit(solution)/shard_map/all_to_all | solution.py:60
  89.4 36.5 %collective-permute-start.3 = (bf16[32,4096]{1,0:T(8,128)(2,1)}, bf16[32,4096]{1,0:T(8,128)(2,1)S(1)}, u32[]{:S(2)}, u32[]{:S(2)}) collective-permute-start(bf16[32,4096]{1,0:T(8,128)(2,1)} %get-tuple-element.23), channel_id=1, source_target_pairs={{0,1},{1,0},{2,3},{3,2},{4,5},{5,4},{6,7},{7,6},{8,9},{9,8},{10,11... | collective-permute-start | bytes 786440 | tf_op jit(solution)/shard_map/ppermute | solution.py:28
  92.4 22.1 %collective-permute-start.19 = (bf16[64,2048]{1,0:T(8,128)(2,1)S(1)}, bf16[64,2048]{1,0:T(8,128)(2,1)}, u32[]{:S(2)}, u32[]{:S(2)}) collective-permute-start(bf16[64,2048]{1,0:T(8,128)(2,1)S(1)} %add_convert_fusion), channel_id=1, source_target_pairs={{0,16},{8,24},{16,0},{24,8},{1,17},{9,25},{17,1},{25,9},{2,18},{10... | collective-permute-start | bytes 786440 | tf_op jit(solution)/shard_map/ppermute | solution.py:28
  93.9 32.0 %copy-start.2 = (bf16[32,4096]{1,0:T(8,128)(2,1)S(1)}, bf16[32,4096]{1,0:T(8,128)(2,1)}, u32[]{:S(2)}) copy-start(bf16[32,4096]{1,0:T(8,128)(2,1)} %get-tuple-element.22.refs_13_) | copy-start | bytes 786436
  95.9 29.9 %collective-permute-start.5 = (bf16[32,4096]{1,0:T(8,128)(2,1)S(1)}, bf16[32,4096]{1,0:T(8,128)(2,1)S(1)}, u32[]{:S(2)}, u32[]{:S(2)}) collective-permute-start(bf16[32,4096]{1,0:T(8,128)(2,1)S(1)} %add_convert_fusion.3), channel_id=1, source_target_pairs={{0,2},{1,3},{2,0},{3,1},{4,6},{5,7},{6,4},{7,5},{8,10},{9,11},{10,... | collective-permute-start | bytes 786440 | tf_op jit(solution)/shard_map/ppermute | solution.py:28
  101.8 24.0 %collective-permute-start.7 = (bf16[32,4096]{1,0:T(8,128)(2,1)S(1)}, bf16[32,4096]{1,0:T(8,128)(2,1)S(1)}, u32[]{:S(2)}, u32[]{:S(2)}) collective-permute-start(bf16[32,4096]{1,0:T(8,128)(2,1)S(1)} %add_convert_fusion.2), channel_id=1, source_target_pairs={{0,4},{1,5},{2,6},{3,7},{4,0},{5,1},{6,2},{7,3},{8,12},{9,13},{10,... | collective-permute-start | bytes 786440 | tf_op jit(solution)/shard_map/ppermute | solution.py:28
  105.9 19.9 %all-to-all-start.1 = ((bf16[16,32,128]{2,1,0:T(8,128)(2,1)}), bf16[16,32,128]{2,1,0:T(8,128)(2,1)S(1)}, u32[]{:S(2)}, u32[]{:S(2)}) async-start(bf16[16,32,128]{2,1,0:T(8,128)(2,1)} %broadcast_in_dim.3), calls=%async_computation.1 | async-start | bytes 262144 | tf_op jit(solution)/shard_map/all_to_all | solution.py:62
  110.7 15.1 %collective-permute-start.9 = (bf16[32,4096]{1,0:T(8,128)(2,1)}, bf16[32,4096]{1,0:T(8,128)(2,1)S(1)}, u32[]{:S(2)}, u32[]{:S(2)}) collective-permute-start(bf16[32,4096]{1,0:T(8,128)(2,1)} %add_convert_fusion.1), channel_id=1, source_target_pairs={{0,6},{1,7},{2,4},{3,5},{4,2},{5,3},{6,0},{7,1},{8,14},{9,15},{10,... | collective-permute-start | bytes 786440 | tf_op jit(solution)/shard_map/ppermute | solution.py:28
  125.8 3.4 %collective-permute-start.21 = (bf16[512,128]{1,0:T(8,128)(2,1)S(1)}, bf16[512,128]{1,0:T(8,128)(2,1)S(1)}, u32[]{:S(2)}, u32[]{:S(2)}) collective-permute-start(bf16[512,128]{1,0:T(8,128)(2,1)S(1)} %bitcast.26), channel_id=1, source_target_pairs={{0,8},{8,0},{1,9},{9,1},{2,10},{10,2},{3,11},{11,3},{4,12},{12,4},... | collective-permute-start | bytes 393224 | tf_op jit(solution)/shard_map/ppermute | solution.py:28
